TPU v7x, 32 devices: a whole 2x2x4 slice. The times are simulated.
32 devices in a mesh: fsdp: 4 (over y, core), dp: 8 (over z, x).
Axes of the slice: x: 2, y: 2, z: 4, core: 2. Of those that a mesh axis runs over, the one named last changes fastest.
Arguments:
- tokens: bfloat16 [8, 2048, 768], P('fsdp', 'dp'), may hold values from -6 to 6
- segments: int32 [8, 2048], P('fsdp'), may hold values from 0 to 2, never falling along the last dimension, each value on 1 to 2000 neighbouring positions
- ln1_gain: bfloat16 [768], P('fsdp'), may hold values from 0.5 to 1.5
- ln1_bias: bfloat16 [768], P('fsdp'), may hold values from -1.75 to 1.75
- w_query: bfloat16 [768, 768], P('fsdp'), may hold values from -0.21875 to 0.21875
- w_key: bfloat16 [768, 768], P('fsdp'), may hold values from -0.21875 to 0.21875
- w_value: bfloat16 [768, 768], P('fsdp'), may hold values from -0.21875 to 0.21875
- shift_taps: bfloat16 [64, 768], P(None, 'fsdp'), may hold values from -0.75 to 0.75
- ssm_rate: bfloat16 [12, 32], P('fsdp'), may hold values from 0.0009994507 to 0.099609375
- ssm_freq: bfloat16 [12, 32], P('fsdp'), may hold values from -0.29882812 to 0.29882812
- ssm_coef: bfloat16 [2, 12, 32], P(None, 'fsdp'), may hold values from -0.01171875 to 0.01171875
- ssm_skip: bfloat16 [12], P('fsdp'), may hold values from -0.625 to 0.625
- w_out: bfloat16 [768, 768], P('fsdp'), may hold values from -0.21875 to 0.21875
- ln2_gain: bfloat16 [768], P('fsdp'), may hold values from 0.5 to 1.5
- ln2_bias: bfloat16 [768], P('fsdp'), may hold values from -1.75 to 1.75
- w_up: bfloat16 [768, 3072], P('fsdp'), may hold values from -0.21875 to 0.21875
- w_down: bfloat16 [3072, 768], P('fsdp'), may hold values from -0.109375 to 0.109375
- cotangent: bfloat16 [8, 2048, 768], P('fsdp', 'dp'), may hold values from -6 to 6
Outputs:
- output: bfloat16 [8, 2048, 768], P('fsdp', 'dp')
- input_grad: bfloat16 [8, 2048, 768], P('fsdp', 'dp')
- ln1_gain_grad: float32 [768], P('fsdp')
- ln1_bias_grad: float32 [768], P('fsdp')
- w_query_grad: float32 [768, 768], P('fsdp')
- w_key_grad: float32 [768, 768], P('fsdp')
- w_value_grad: float32 [768, 768], P('fsdp')
- shift_taps_grad: float32 [64, 768], P(None, 'fsdp')
- ssm_rate_grad: float32 [12, 32], P('fsdp')
- ssm_freq_grad: float32 [12, 32], P('fsdp')
- ssm_coef_grad: float32 [2, 12, 32], P(None, 'fsdp')
- ssm_skip_grad: float32 [12], P('fsdp')
- w_out_grad: float32 [768, 768], P('fsdp')
- ln2_gain_grad: float32 [768], P('fsdp')
- ln2_bias_grad: float32 [768], P('fsdp')
- w_up_grad: float32 [768, 3072], P('fsdp')
- w_down_grad: float32 [3072, 768], P('fsdp')
Inputs may be any that keep to these rules, and one draw needn't show every extreme that they name: `segments`: along each row the document numbers never fall; each document has 1 to 2000 tokens and some document in each row exactly 2000.
All inputs are finite; a program needn't handle non-finite values.
Results may differ from a plain program's by a relative error of at most 0.014.
Values may be sent and summed in bfloat16 or wider, within the bound.
No kernel may reach another device: no remote copies, remote signals or barrier semaphores. Data moves between devices by JAX's collectives and lax.ppermute only.
A program may use at most 256 MiB of HBM per device.

v0:
```python
import jax
import jax.numpy as jnp
from jax import lax
from jax.sharding import PartitionSpec as P

SHIFT = 64
HOPS = 8
KW = 2304


epsilon = 1e-05


def passed_along(value, axis, steps):
    count = lax.axis_size(axis)
    leading, last = (max(0, -steps), min(count, count - steps))
    return lax.ppermute(value, axis, [(source, source + steps) for source in range(leading, last)])


def layer_norm(inputs, scales, offsets):
    row_mean = jnp.mean(inputs, axis=-1, keepdims=True)
    centered = inputs - row_mean
    spread = jnp.mean(centered * centered, axis=-1, keepdims=True)
    return centered * lax.rsqrt(spread + epsilon) * scales + offsets


def kernel_table(decay_rate, frequency, coefficients, skip_gain):
    lag_values = jnp.arange(KW).astype(jnp.float32)
    decays = jnp.exp(-decay_rate[:, :, None] * lag_values)
    angles = frequency[:, :, None] * lag_values
    oscillation = coefficients[0][:, :, None] * jnp.cos(angles) - coefficients[1][
        :, :, None
    ] * jnp.sin(angles)
    first_lag = (jnp.arange(KW) == 0).astype(jnp.float32)
    return jnp.sum(decays * oscillation, axis=1) + skip_gain[:, None] * first_lag


def toeplitz_rows(kernel_row, row_count):
    length = row_count + KW - 1
    extended = jnp.concatenate([jnp.zeros((row_count - 1,), jnp.float32), kernel_row])[::-1]
    tiled = jnp.tile(extended, row_count + 1)
    band_flat = lax.slice_in_dim(tiled, row_count - 1, row_count - 1 + row_count * (length - 1))
    return band_flat.reshape(row_count, length - 1)[:, :KW]


def shift_forward(key_ext, taps_full, seg_ext):
    row_count = key_ext.shape[1] - (SHIFT - 1)
    seg_now = seg_ext[:, SHIFT - 1 :]

    def one_tap(running, tap_lag):
        first_row = SHIFT - 1 - tap_lag
        shifted_part = lax.dynamic_slice_in_dim(key_ext, first_row, row_count, 1)
        same_doc = lax.dynamic_slice_in_dim(seg_ext, first_row, row_count, 1) == seg_now
        weight = lax.dynamic_index_in_dim(taps_full, tap_lag, 0, keepdims=False)
        return (running + jnp.where(same_doc[..., None], shifted_part, 0.0) * weight, None)

    start_sum = jnp.zeros((key_ext.shape[0], row_count, key_ext.shape[2]), jnp.float32)
    running, _ = lax.scan(one_tap, start_sum, jnp.arange(SHIFT))
    return running


def shift_backward(key_ext, taps_full, seg_ext, out_grad):
    row_count = key_ext.shape[1] - (SHIFT - 1)
    seg_now = seg_ext[:, SHIFT - 1 :]

    def one_tap(ext_grad, tap_lag):
        first_row = SHIFT - 1 - tap_lag
        shifted_part = lax.dynamic_slice_in_dim(key_ext, first_row, row_count, 1)
        same_doc = lax.dynamic_slice_in_dim(seg_ext, first_row, row_count, 1) == seg_now
        weight = lax.dynamic_index_in_dim(taps_full, tap_lag, 0, keepdims=False)
        masked = jnp.where(same_doc[..., None], out_grad, 0.0)
        tap_grad = jnp.sum(masked * shifted_part, axis=(0, 1))
        current = lax.dynamic_slice_in_dim(ext_grad, first_row, row_count, 1)
        ext_grad = lax.dynamic_update_slice_in_dim(
            ext_grad, current + masked * weight, first_row, 1
        )
        return (ext_grad, tap_grad)

    ext_grad, tap_grads = lax.scan(one_tap, jnp.zeros_like(key_ext), jnp.arange(SHIFT))
    return (ext_grad, tap_grads)


def head_forward(q_head, k_head, v_head, kernel_row, live_mask):
    kernel_mat = toeplitz_rows(kernel_row, q_head.shape[1])
    scores = jnp.einsum("std,sud->stu", q_head, k_head, preferred_element_type=jnp.float32)
    weights = jnp.where(live_mask, scores * kernel_mat, 0.0).astype(jnp.bfloat16)
    return jnp.einsum("stu,sue->ste", weights, v_head, preferred_element_type=jnp.float32)


def head_backward(q_head, k_head, v_head, kernel_row, live_mask, grad_head):
    row_count = q_head.shape[1]
    kernel_mat, kernel_pull = jax.vjp(
        lambda row_values: toeplitz_rows(row_values, row_count), kernel_row
    )
    scores = jnp.einsum("std,sud->stu", q_head, k_head, preferred_element_type=jnp.float32)
    weights = jnp.where(live_mask, scores * kernel_mat, 0.0).astype(jnp.bfloat16)
    grad_weights = jnp.where(
        live_mask,
        jnp.einsum("ste,sue->stu", grad_head, v_head, preferred_element_type=jnp.float32),
        0.0,
    )
    grad_scores = (grad_weights * kernel_mat).astype(jnp.bfloat16)
    grad_kernel = kernel_pull(jnp.sum(grad_weights * scores, axis=0))[0]
    grad_query = jnp.einsum("stu,sud->std", grad_scores, k_head, preferred_element_type=jnp.float32)
    grad_key = jnp.einsum("stu,std->sud", grad_scores, q_head, preferred_element_type=jnp.float32)
    grad_value = jnp.einsum("stu,ste->sue", weights, grad_head, preferred_element_type=jnp.float32)
    return (grad_query, grad_key, grad_value, grad_kernel)


def shards(
    tokens,
    segments,
    ln1_gain,
    ln1_bias,
    w_query,
    w_key,
    w_value,
    shift_taps,
    ssm_rate,
    ssm_freq,
    ssm_coef,
    ssm_skip,
    w_out,
    ln2_gain,
    ln2_bias,
    w_up,
    w_down,
    cotangent,
):
    gathered = (
        lax.all_gather(ln1_gain, "fsdp", axis=0, tiled=True),
        lax.all_gather(ln1_bias, "fsdp", axis=0, tiled=True),
        lax.all_gather(w_query, "fsdp", axis=0, tiled=True),
        lax.all_gather(w_key, "fsdp", axis=0, tiled=True),
        lax.all_gather(w_value, "fsdp", axis=0, tiled=True),
        lax.all_gather(shift_taps, "fsdp", axis=1, tiled=True),
        lax.all_gather(ssm_rate, "fsdp", axis=0, tiled=True),
        lax.all_gather(ssm_freq, "fsdp", axis=0, tiled=True),
        lax.all_gather(ssm_coef, "fsdp", axis=1, tiled=True),
        lax.all_gather(ssm_skip, "fsdp", axis=0, tiled=True),
        lax.all_gather(w_out, "fsdp", axis=0, tiled=True),
        lax.all_gather(ln2_gain, "fsdp", axis=0, tiled=True),
        lax.all_gather(ln2_bias, "fsdp", axis=0, tiled=True),
        lax.all_gather(w_up, "fsdp", axis=0, tiled=True),
        lax.all_gather(w_down, "fsdp", axis=0, tiled=True),
    )
    (
        gain_one,
        bias_one,
        query_w,
        key_w,
        value_w,
        taps_w,
        rate_full,
        freq_full,
        coef_full,
        skip_full,
        out_w,
        gain_two,
        bias_two,
        up_w,
        down_w,
    ) = gathered
    seq_count, row_count, width = tokens.shape
    heads = rate_full.shape[0]
    head_size = width // heads
    reach_rows = HOPS * row_count
    row_base = lax.axis_index("dp") * row_count
    seg_pad = jnp.concatenate([jnp.full((seq_count, reach_rows), -1, jnp.int32), segments], axis=1)
    seg_window = lax.dynamic_slice_in_dim(seg_pad, row_base, KW, 1)
    seg_query = seg_window[:, reach_rows:]
    seg_shift = lax.dynamic_slice_in_dim(
        seg_pad, row_base + reach_rows - (SHIFT - 1), row_count + SHIFT - 1, 1
    )
    causal = lax.broadcasted_iota(
        jnp.int32, (row_count, KW), 0
    ) + reach_rows >= lax.broadcasted_iota(jnp.int32, (row_count, KW), 1)
    live_mask = (seg_query[:, :, None] == seg_window[:, None, :]) & causal[None]

    def to_heads(tensor):
        return tensor.reshape(tensor.shape[0], tensor.shape[1], heads, head_size).transpose(
            2, 0, 1, 3
        )

    def from_heads(tensor):
        return tensor.transpose(1, 2, 0, 3).reshape(tensor.shape[1], tensor.shape[2], width)

    inputs = tokens.astype(jnp.float32)
    normed, norm_one_pull = jax.vjp(
        layer_norm, inputs, gain_one.astype(jnp.float32), bias_one.astype(jnp.float32)
    )
    act_one = normed.astype(jnp.bfloat16)
    queries = jnp.einsum(
        "std,de->ste", act_one, query_w, preferred_element_type=jnp.float32
    ).astype(jnp.bfloat16)
    key_rows = jnp.einsum("std,de->ste", act_one, key_w, preferred_element_type=jnp.float32).astype(
        jnp.bfloat16
    )
    values = jnp.einsum("std,de->ste", act_one, value_w, preferred_element_type=jnp.float32).astype(
        jnp.bfloat16
    )
    prev_tail = passed_along(key_rows[:, row_count - SHIFT + 1 :, :], "dp", 1)
    key_ext = jnp.concatenate([prev_tail, key_rows], axis=1).astype(jnp.float32)
    taps_full = taps_w.astype(jnp.float32)
    shifted = shift_forward(key_ext, taps_full, seg_shift).astype(jnp.bfloat16)
    pieces = []
    for distance in range(HOPS, 0, -1):
        pieces.append(passed_along((shifted, values), "dp", distance))
    key_window = jnp.concatenate([piece[0] for piece in pieces] + [shifted], axis=1)
    value_window = jnp.concatenate([piece[1] for piece in pieces] + [values], axis=1)
    kernel_rows, kernel_pull = jax.vjp(
        kernel_table,
        rate_full.astype(jnp.float32),
        freq_full.astype(jnp.float32),
        coef_full.astype(jnp.float32),
        skip_full.astype(jnp.float32),
    )
    q_heads = to_heads(queries)
    k_heads = to_heads(key_window)
    v_heads = to_heads(value_window)
    mixed_heads = lax.map(
        lambda head_item: head_forward(
            head_item[0], head_item[1], head_item[2], head_item[3], live_mask
        ),
        (q_heads, k_heads, v_heads, kernel_rows),
    )
    mixed = from_heads(mixed_heads).astype(jnp.bfloat16)
    resid = inputs + jnp.einsum("std,de->ste", mixed, out_w, preferred_element_type=jnp.float32)
    normed_two, norm_two_pull = jax.vjp(
        layer_norm, resid, gain_two.astype(jnp.float32), bias_two.astype(jnp.float32)
    )
    act_two = normed_two.astype(jnp.bfloat16)
    up_rows = jnp.einsum("std,df->stf", act_two, up_w, preferred_element_type=jnp.float32)
    gelu_rows, gelu_pull = jax.vjp(lambda entries: jax.nn.gelu(entries, approximate=True), up_rows)
    hidden = gelu_rows.astype(jnp.bfloat16)
    output = (
        resid + jnp.einsum("stf,fd->std", hidden, down_w, preferred_element_type=jnp.float32)
    ).astype(jnp.bfloat16)
    regathered = (
        lax.all_gather(ln1_gain, "fsdp", axis=0, tiled=True),
        lax.all_gather(ln1_bias, "fsdp", axis=0, tiled=True),
        lax.all_gather(w_query, "fsdp", axis=0, tiled=True),
        lax.all_gather(w_key, "fsdp", axis=0, tiled=True),
        lax.all_gather(w_value, "fsdp", axis=0, tiled=True),
        lax.all_gather(shift_taps, "fsdp", axis=1, tiled=True),
        lax.all_gather(ssm_rate, "fsdp", axis=0, tiled=True),
        lax.all_gather(ssm_freq, "fsdp", axis=0, tiled=True),
        lax.all_gather(ssm_coef, "fsdp", axis=1, tiled=True),
        lax.all_gather(ssm_skip, "fsdp", axis=0, tiled=True),
        lax.all_gather(w_out, "fsdp", axis=0, tiled=True),
        lax.all_gather(ln2_gain, "fsdp", axis=0, tiled=True),
        lax.all_gather(ln2_bias, "fsdp", axis=0, tiled=True),
        lax.all_gather(w_up, "fsdp", axis=0, tiled=True),
        lax.all_gather(w_down, "fsdp", axis=0, tiled=True),
    )
    query_b, key_b, value_b, taps_b, out_b, up_b, down_b = (
        regathered[2],
        regathered[3],
        regathered[4],
        regathered[5],
        regathered[10],
        regathered[13],
        regathered[14],
    )
    taps_back = taps_b.astype(jnp.float32)
    down_grad = jnp.einsum("stf,std->fd", hidden, cotangent, preferred_element_type=jnp.float32)
    hidden_grad = jnp.einsum("std,fd->stf", cotangent, down_b, preferred_element_type=jnp.float32)
    up_grad_rows = gelu_pull(hidden_grad)[0].astype(jnp.bfloat16)
    up_grad = jnp.einsum("std,stf->df", act_two, up_grad_rows, preferred_element_type=jnp.float32)
    act_two_grad = jnp.einsum("stf,df->std", up_grad_rows, up_b, preferred_element_type=jnp.float32)
    resid_part, gain_two_grad, bias_two_grad = norm_two_pull(act_two_grad)
    resid_grad = cotangent.astype(jnp.float32) + resid_part
    resid_low = resid_grad.astype(jnp.bfloat16)
    out_grad = jnp.einsum("ste,std->ed", mixed, resid_low, preferred_element_type=jnp.float32)
    mixed_grad = jnp.einsum(
        "std,ed->ste", resid_low, out_b, preferred_element_type=jnp.float32
    ).astype(jnp.bfloat16)
    grad_heads = to_heads(mixed_grad)

    def block_of(tensor, distance):
        offset = (HOPS - distance) * row_count
        return tensor[:, offset : offset + row_count]

    head_grads = lax.map(
        lambda head_item: head_backward(
            head_item[0], head_item[1], head_item[2], head_item[3], live_mask, head_item[4]
        ),
        (q_heads, k_heads, v_heads, kernel_rows, grad_heads),
    )
    query_grad_rows = from_heads(head_grads[0]).astype(jnp.bfloat16)
    key_window_grad = from_heads(head_grads[1])
    value_window_grad = from_heads(head_grads[2])
    rate_grad, freq_grad, coef_grad, skip_grad = kernel_pull(head_grads[3])
    shifted_grad = block_of(key_window_grad, 0)
    values_grad = block_of(value_window_grad, 0)
    for distance in range(1, HOPS + 1):
        returned = (
            passed_along(
                block_of(key_window_grad, distance).astype(jnp.bfloat16), "dp", -distance
            ).astype(jnp.float32),
            passed_along(
                block_of(value_window_grad, distance).astype(jnp.bfloat16), "dp", -distance
            ).astype(jnp.float32),
        )
        shifted_grad = shifted_grad + returned[0]
        values_grad = values_grad + returned[1]
    ext_grad, taps_grad = shift_backward(key_ext, taps_back, seg_shift, shifted_grad)
    tail_grad = passed_along(ext_grad[:, : SHIFT - 1, :].astype(jnp.bfloat16), "dp", -1).astype(
        jnp.float32
    )
    tail_padded = jnp.concatenate(
        [jnp.zeros((seq_count, row_count - SHIFT + 1, width), jnp.float32), tail_grad], axis=1
    )
    key_grad_rows = (ext_grad[:, SHIFT - 1 :, :] + tail_padded).astype(jnp.bfloat16)
    value_grad_rows = values_grad.astype(jnp.bfloat16)
    query_grad = jnp.einsum(
        "std,ste->de", act_one, query_grad_rows, preferred_element_type=jnp.float32
    )
    key_grad = jnp.einsum("std,ste->de", act_one, key_grad_rows, preferred_element_type=jnp.float32)
    value_grad = jnp.einsum(
        "std,ste->de", act_one, value_grad_rows, preferred_element_type=jnp.float32
    )
    act_one_grad = (
        jnp.einsum("ste,de->std", query_grad_rows, query_b, preferred_element_type=jnp.float32)
        + jnp.einsum("ste,de->std", key_grad_rows, key_b, preferred_element_type=jnp.float32)
        + jnp.einsum("ste,de->std", value_grad_rows, value_b, preferred_element_type=jnp.float32)
    )
    input_part, gain_one_grad, bias_one_grad = norm_one_pull(act_one_grad)
    input_grad = (resid_grad + input_part).astype(jnp.bfloat16)
    owned = (
        lax.psum_scatter(gain_one_grad, "fsdp", scatter_dimension=0, tiled=True),
        lax.psum_scatter(bias_one_grad, "fsdp", scatter_dimension=0, tiled=True),
        lax.psum_scatter(query_grad, "fsdp", scatter_dimension=0, tiled=True),
        lax.psum_scatter(key_grad, "fsdp", scatter_dimension=0, tiled=True),
        lax.psum_scatter(value_grad, "fsdp", scatter_dimension=0, tiled=True),
        lax.psum_scatter(taps_grad, "fsdp", scatter_dimension=1, tiled=True),
        lax.psum_scatter(rate_grad, "fsdp", scatter_dimension=0, tiled=True),
        lax.psum_scatter(freq_grad, "fsdp", scatter_dimension=0, tiled=True),
        lax.psum_scatter(coef_grad, "fsdp", scatter_dimension=1, tiled=True),
        lax.psum_scatter(skip_grad, "fsdp", scatter_dimension=0, tiled=True),
        lax.psum_scatter(out_grad, "fsdp", scatter_dimension=0, tiled=True),
        lax.psum_scatter(gain_two_grad, "fsdp", scatter_dimension=0, tiled=True),
        lax.psum_scatter(bias_two_grad, "fsdp", scatter_dimension=0, tiled=True),
        lax.psum_scatter(up_grad, "fsdp", scatter_dimension=0, tiled=True),
        lax.psum_scatter(down_grad, "fsdp", scatter_dimension=0, tiled=True),
    )
    summed = lax.psum(
        (
            owned[0],
            owned[1],
            owned[2],
            owned[3],
            owned[4],
            owned[5],
            owned[6],
            owned[7],
            owned[8],
            owned[9],
            owned[10],
            owned[11],
            owned[12],
            owned[13],
            owned[14],
        ),
        "dp",
    )
    return (
        output,
        input_grad,
        summed[0],
        summed[1],
        summed[2],
        summed[3],
        summed[4],
        summed[5],
        summed[6],
        summed[7],
        summed[8],
        summed[9],
        summed[10],
        summed[11],
        summed[12],
        summed[13],
        summed[14],
    )


def solution(mesh):
    return jax.shard_map(
        shards,
        mesh=mesh,
        in_specs=(
            P("fsdp", "dp", None),
            P("fsdp", None),
            P("fsdp"),
            P("fsdp"),
            P("fsdp", None),
            P("fsdp", None),
            P("fsdp", None),
            P(None, "fsdp"),
            P("fsdp", None),
            P("fsdp", None),
            P(None, "fsdp", None),
            P("fsdp"),
            P("fsdp", None),
            P("fsdp"),
            P("fsdp"),
            P("fsdp", None),
            P("fsdp", None),
            P("fsdp", "dp", None),
        ),
        out_specs=(
            P("fsdp", "dp", None),
            P("fsdp", "dp", None),
            P("fsdp"),
            P("fsdp"),
            P("fsdp", None),
            P("fsdp", None),
            P("fsdp", None),
            P(None, "fsdp"),
            P("fsdp", None),
            P("fsdp", None),
            P(None, "fsdp", None),
            P("fsdp"),
            P("fsdp", None),
            P("fsdp"),
            P("fsdp"),
            P("fsdp", None),
            P("fsdp", None),
        ),
        check_vma=False,
    )
```

profile of v0, /device:TPU:0, one launch (start us, length us, event | category | flops | bytes accessed | tf_op | source)
XLA Modules:
  0.0 3321.2 jit_solution(2754218657446344280)
XLA Ops:
  15.3 9.1 all-reduce.24
  24.5 5.1 all-gather.1
  29.6 5.1 all-gather.2
  34.7 5.1 all_gather.58
  40.3 14.2 fusion.78
  57.9 5.1 collective-permute-start.14
  63.0 5.4 all-gather
  69.3 5.2 collective-permute-start.13
  95.1 484.3 %while.58 = (s32[]{:T(128)}, f32[2,256,768]{2,1,0:T(8,128)}, s32[64]{0:T(128)S(1)}, s32[2,319]{1,0:T(2,128)S(1)}, s32[2,256]{1,0:T(2,128)S(1)}, /*index=5*/f32[2...) while((s32[]{:T(128)}, f32[2,256,768]{2,1,0:T(8,128)}, ...), condition=%wide.region_3.4_spmd.clone, body=%wide.region_2.3_spmd.clone.sunk | while | flops 1573386 | bytes 4733167 | solution.py:58
  582.7 57.5 %collective-permute-start.15 = (bf16[2,256,768]{2,1,0:T(8,128)(2,1)}, bf16[2,256,768]{2,1,0:T(8,128)(2,1)S(1)}, u32[]{:S(2)}, u32[]{:S(2)}) collective-permute-start(bf16[2,256,768]{2,1,0:T(8,128)(2,1)} %convolution_convert_fusion.1), channel_id=1, source_target_pairs={{0,2},{1,3},{2,4},{3,5},{4,6},{5,7},{8,10},{9,11},{10,12},{11,13},... | collective-permute-start | bytes 2359304 | tf_op jit(solution)/shard_map/ppermute | solution.py:17
  642.3 26.7 collective-permute-start.16
  688.2 53.6 %collective-permute-start.5 = (bf16[2,256,768]{1,2,0:T(8,128)(2,1)}, bf16[2,256,768]{1,2,0:T(8,128)(2,1)}, u32[]{:S(2)}, u32[]{:S(2)}) collective-permute-start(bf16[2,256,768]{1,2,0:T(8,128)(2,1)} %copy.136), channel_id=1, source_target_pairs={{0,4},{1,5},{2,6},{3,7},{8,12},{9,13},{10,14},{11,15},{16,20},{17,... | collective-permute-start | bytes 2359304 | tf_op jit(solution)/shard_map/ppermute | solution.py:17
  747.2 10.5 copy.138
  757.7 6.6 copy.141
  770.7 5.4 collective-permute-done.6
  777.3 13.9 collective-permute-done.7
  796.9 171.6 %while.56 = (s32[]{:T(128)}, bf16[12,2,256,64]{2,3,0,1:T(8,128)(2,1)}, bf16[12,2,256,64]{2,3,1,0:T(8,128)(2,1)}, bf16[12,2,2304,64]{2,3,1,0:T(8,128)(2,1)}, f32[...) while((s32[]{:T(128)}, ...), condition=%wide.region_6.7_spmd.clone, body=%wide.region_5.6_spmd.clone.sunk | while | flops 307888128 | bytes 29884536 | solution.py:221
  971.5 7.2 fusion.69
  978.7 8.8 fusion.56
  999.8 601.9 %while.57 = (s32[]{:T(128)}, bf16[12,2,256,64]{2,3,0,1:T(8,128)(2,1)}, f32[12,2,2304,64]{2,3,0,1:T(8,128)}, f32[12,2,2304,64]{2,3,0,1:T(8,128)}, f32[12,2304]{1,...) while((s32[]{:T(128)}, ...), condition=%wide.region_14.15_spmd.clone, body=%wide.region_11.14_spmd.clone.sunk | while | flops 771555072 | bytes 123129032 | solution.py:284
  1022.0 5.6 multiply_reduce_fusion.9
  1029.6 4.9 reshape.267
  1071.9 5.6 multiply_reduce_fusion.9
  1079.5 4.9 reshape.267
  1121.3 5.6 multiply_reduce_fusion.9
  1128.8 4.9 reshape.267
  1170.6 5.6 multiply_reduce_fusion.9
  1178.1 4.9 reshape.267
  1219.9 5.6 multiply_reduce_fusion.9
  1227.4 4.9 reshape.267
  1269.2 5.6 multiply_reduce_fusion.9
  1276.7 4.9 reshape.267
  1318.5 5.6 multiply_reduce_fusion.9
  1326.1 4.9 reshape.267
  1367.8 5.6 multiply_reduce_fusion.9
  1375.3 4.9 reshape.267
  1417.0 5.6 multiply_reduce_fusion.9
  1424.6 4.9 reshape.267
  1466.3 5.6 multiply_reduce_fusion.9
  1473.9 4.9 reshape.267
  1515.6 5.6 multiply_reduce_fusion.9
  1523.1 4.9 reshape.267
  1564.9 5.6 multiply_reduce_fusion.9
  1605.7 9.7 bitcast_convert_fusion
  1623.3 46.6 %collective-permute-done.26 = bf16[2,256,768]{1,2,0:T(8,128)(2,1)S(1)} collective-permute-done((bf16[2,256,768]{1,2,0:T(8,128)(2,1)S(1)}, bf16[2,256,768]{1,2,0:T(8,128)(2,1)S(1)}, u32[]{:S(2)}, u32[]{:S(2)}) %collective-permute-start.26) | collective-permute-done | bytes 786464 | tf_op jit(solution)/shard_map/ppermute | solution.py:17
  1673.8 28.5 collective-permute-done.17
  1708.7 33.2 collective-permute-done.21
  1743.2 42.8 %collective-permute-done.20 = bf16[2,256,768]{1,2,0:T(8,128)(2,1)S(1)} collective-permute-done((bf16[2,256,768]{1,2,0:T(8,128)(2,1)S(1)}, bf16[2,256,768]{1,2,0:T(8,128)(2,1)S(1)}, u32[]{:S(2)}, u32[]{:S(2)}) %collective-permute-start.20) | collective-permute-done | bytes 786464 | tf_op jit(solution)/shard_map/ppermute | solution.py:17
  1796.6 12.7 collective-permute-done.31
  1809.3 67.7 %collective-permute-done.30 = bf16[2,256,768]{1,2,0:T(8,128)(2,1)} collective-permute-done((bf16[2,256,768]{1,2,0:T(8,128)(2,1)}, bf16[2,256,768]{1,2,0:T(8,128)(2,1)}, u32[]{:S(2)}, u32[]{:S(2)}) %collective-permute-start.30) | collective-permute-done | bytes 786464 | tf_op jit(solution)/shard_map/ppermute | solution.py:17
  1877.0 27.2 collective-permute-done.29
  1904.2 32.0 collective-permute-done.27
  1945.5 885.5 %while.55 = (s32[]{:T(128)}, f32[2,319,768]{2,1,0:T(8,128)}, f32[64,768]{1,0:T(8,128)}, s32[64]{0:T(128)}, s32[2,319]{1,0:T(2,128)S(1)}, /*index=5*/s32[2,256]{1...) while((s32[]{:T(128)}, f32[2,319,768]{2,1,0:T(8,128)}, ...), condition=%wide.region_17.18_spmd, body=%wide.region_15.17_spmd.sunk | while | flops 1965833 | bytes 9467133 | solution.py:79
  2833.3 7.4 collective-permute-done.25
  2846.7 10.0 convolution_bitcast_fusion.3
  2858.1 7.5 convolution_bitcast_fusion.4
  2867.8 7.0 reduce-scatter.12.cloned.1.call-done
  2874.8 81.1 %reduce-scatter.20.cloned.1.call-done = f32[768,768]{1,0:T(8,128)} async-done(((f32[3072,768]{1,0:T(8,128)}), f32[768,768]{1,0:T(8,128)}) %reduce-scatter.20.cloned.1.call-update) | async-done | bytes 2359312 | tf_op jit(solution)/shard_map/reduce_scatter | solution.py:345
  2955.8 80.9 %reduce-scatter.18.cloned.1.call-done = f32[192,3072]{1,0:T(8,128)} async-done(((f32[768,3072]{1,0:T(8,128)}), f32[192,3072]{1,0:T(8,128)}) %reduce-scatter.18.cloned.1.call-update) | async-done | bytes 2359312 | tf_op jit(solution)/shard_map/reduce_scatter | solution.py:344
  3038.3 17.6 fusion.75
  3056.9 8.9 add_convert_fusion.2
  3070.8 11.4 all-reduce.23
  3086.6 41.8 %all-reduce.21 = (f32[192]{0:T(256)}, f32[192]{0:T(256)}, f32[64,192]{1,0:T(8,128)}, f32[3,32]{1,0:T(4,128)}, f32[3,32]{1,0:T(4,128)}, /*index=5*/f32[2,3,32]{2,...) all-reduce(f32[192]{0:T(256)S(1)} %dynamic-slice.6, ...), channel_id=1, replica_groups=mesh['fsdp'=4,'dp'=8] {'dp'}, use_global_device_ids=true, to_apply=%region_22.23 | all-reduce | flops 13443 | bytes 107544 | tf_op jit(solution)/shard_map/psum | solution.py:347
  3128.4 176.5 %all-reduce.27.cloned.1.call-done = (f32[192,768]{1,0:T(8,128)}, f32[192,768]{1,0:T(8,128)}, f32[192,768]{1,0:T(8,128)}, f32[192,768]{1,0:T(8,128)}, f32[192,3072]{1,0:T(8,128)}, /*index=5*/f32[768,768]{1,0:T(8,128)}) async-done(((f32[192,768]{1,0:T(8,128)}, f32[192,768]{1,0:T(8,128)}, f32[192,768]{1,0:T(8,128)}, f32[192,768]{1,0:T(8,128)}, f32[192,3072]{1,0:T(8,128)}, /*index=5*/f32[768,768]{1,0:T(8,128)}), ...) | async-done | bytes 7077904 | tf_op jit(solution)/shard_map/psum | solution.py:347
  (1555 shorter events, 1760.5 us)
Async XLA Ops:
  7.2 47.5 %all-gather.14.cloned.1.call-start = ((), (), s32[]{:S(2)}) async-start(), calls=%async_computation.9 | async-start | bytes 1474560 | tf_op jit(solution)/shard_map/all_gather | solution.py:135
  8.0 71.0 %all-gather.12.cloned.1.call-start = ((), (), s32[]{:S(2)}) async-start(), calls=%async_computation.8 | async-start | bytes 1474560 | tf_op jit(solution)/shard_map/all_gather | solution.py:134
  8.8 74.5 %all-gather.10.cloned.1.call-start = ((), (), s32[]{:S(2)}) async-start(), calls=%async_computation.7 | async-start | bytes 1474560 | tf_op jit(solution)/shard_map/all_gather | solution.py:133
  9.5 958.9 %all-gather.16.cloned.1.call-start = ((), (), s32[]{:S(2)}) async-start(), calls=%async_computation.10 | async-start | bytes 1474560 | tf_op jit(solution)/shard_map/all_gather | solution.py:141
  10.1 961.3 %all-gather.18.cloned.1.call-start = ((), (), s32[]{:S(2)}) async-start(), calls=%async_computation.11 | async-start | bytes 5898240 | tf_op jit(solution)/shard_map/all_gather | solution.py:144
  10.7 968.0 %all-gather.20.cloned.1.call-start = ((), (), s32[]{:S(2)}) async-start(), calls=%async_computation.12 | async-start | bytes 5898240 | tf_op jit(solution)/shard_map/all_gather | solution.py:145
  11.3 2856.5 %reduce-scatter.16.cloned.1.call-start = ((), (), s32[]{:S(2)}) async-start(), calls=%async_computation.16 | async-start | bytes 2949120 | tf_op jit(solution)/shard_map/reduce_scatter | solution.py:341
  13.7 69.6 %copy-start.45 = (f32[2,256]{1,0:T(2,128)}, f32[2,256]{1,0:T(2,128)S(1)}, u32[]{:S(2)}) copy-start(f32[2,256]{1,0:T(2,128)S(1)} %broadcast_multiply_fusion.1) | copy-start | bytes 6148
  24.5 966.5 %copy-start.58 = (f32[768]{0:T(1024)}, f32[768]{0:T(1024)S(1)}, u32[]{:S(2)}) copy-start(f32[768]{0:T(1024)S(1)} %convert_element_type.213) | copy-start | bytes 9220
  24.5 946.9 %copy-start.74 = (f32[768]{0:T(1024)}, f32[768]{0:T(1024)S(1)}, u32[]{:S(2)}) copy-start(f32[768]{0:T(1024)S(1)} %convert_element_type.214) | copy-start | bytes 9220
  57.9 35.6 %collective-permute-start.14 = (bf16[2,256,768]{2,1,0:T(8,128)(2,1)}, bf16[2,256,768]{2,1,0:T(8,128)(2,1)}, u32[]{:S(2)}, u32[]{:S(2)}) collective-permute-start(bf16[2,256,768]{2,1,0:T(8,128)(2,1)} %convolution_convert_fusion.1), channel_id=1, source_target_pairs={{0,3},{1,4},{2,5},{3,6},{4,7},{8,11},{9,12},{10,13},{11,14},{12,15... | collective-permute-start | bytes 2359304 | tf_op jit(solution)/shard_map/ppermute | solution.py:17
  69.3 608.0 %collective-permute-start.13 = (bf16[2,256,768]{2,1,0:T(8,128)(2,1)}, bf16[2,256,768]{2,1,0:T(8,128)(2,1)}, u32[]{:S(2)}, u32[]{:S(2)}) collective-permute-start(bf16[2,256,768]{2,1,0:T(8,128)(2,1)} %convolution_convert_fusion.1), channel_id=1, source_target_pairs={{0,4},{1,5},{2,6},{3,7},{8,12},{9,13},{10,14},{11,15},{16,20},{17,... | collective-permute-start | bytes 2359304 | tf_op jit(solution)/shard_map/ppermute | solution.py:17
  74.6 600.0 %collective-permute-start.12 = (bf16[2,256,768]{2,1,0:T(8,128)(2,1)}, bf16[2,256,768]{2,1,0:T(8,128)(2,1)}, u32[]{:S(2)}, u32[]{:S(2)}) collective-permute-start(bf16[2,256,768]{2,1,0:T(8,128)(2,1)} %convolution_convert_fusion.1), channel_id=1, source_target_pairs={{0,5},{1,6},{2,7},{8,13},{9,14},{10,15},{16,21},{17,22},{18,23},{2... | collective-permute-start | bytes 2359304 | tf_op jit(solution)/shard_map/ppermute | solution.py:17
  76.7 594.4 %collective-permute-start.11 = (bf16[2,256,768]{2,1,0:T(8,128)(2,1)}, bf16[2,256,768]{2,1,0:T(8,128)(2,1)}, u32[]{:S(2)}, u32[]{:S(2)}) collective-permute-start(bf16[2,256,768]{2,1,0:T(8,128)(2,1)} %convolution_convert_fusion.1), channel_id=1, source_target_pairs={{0,6},{1,7},{8,14},{9,15},{16,22},{17,23},{24,30},{25,31}} | collective-permute-start | bytes 2359304 | tf_op jit(solution)/shard_map/ppermute | solution.py:17
  82.0 6.3 collective-permute-start
  88.2 554.1 %collective-permute-start.10 = (bf16[2,256,768]{2,1,0:T(8,128)(2,1)}, bf16[2,256,768]{2,1,0:T(8,128)(2,1)}, u32[]{:S(2)}, u32[]{:S(2)}) collective-permute-start(bf16[2,256,768]{2,1,0:T(8,128)(2,1)} %convolution_convert_fusion.1), channel_id=1, source_target_pairs={{0,7},{8,15},{16,23},{24,31}} | collective-permute-start | bytes 2359304 | tf_op jit(solution)/shard_map/ppermute | solution.py:17
  93.5 489.2 %collective-permute-start.9 = (bf16[2,256,768]{2,1,0:T(8,128)(2,1)}, bf16[2,256,768]{2,1,0:T(8,128)(2,1)}, u32[]{:S(2)}, u32[]{:S(2)}) collective-permute-start(bf16[2,256,768]{2,1,0:T(8,128)(2,1)} %convolution_convert_fusion.1), channel_id=1, source_target_pairs={} | collective-permute-start | bytes 2359304 | tf_op jit(solution)/shard_map/ppermute | solution.py:17
  579.4 91.7 %copy-start.1 = (f32[2,319,768]{2,1,0:T(8,128)}, f32[2,319,768]{2,1,0:T(8,128)S(1)}, u32[]{:S(2)}) copy-start(f32[2,319,768]{2,1,0:T(8,128)S(1)} %get-tuple-element.1145) | copy-start | bytes 5879812
  579.4 91.7 %copy-start.34 = (s32[2,256]{1,0:T(2,128)}, s32[2,256]{1,0:T(2,128)S(1)}, u32[]{:S(2)}) copy-start(s32[2,256]{1,0:T(2,128)S(1)} %get-tuple-element.1230) | copy-start | bytes 6148
  579.4 91.7 %copy-start.37 = (s32[2,319]{1,0:T(2,128)}, s32[2,319]{1,0:T(2,128)S(1)}, u32[]{:S(2)}) copy-start(s32[2,319]{1,0:T(2,128)S(1)} %get-tuple-element.1233) | copy-start | bytes 7660
  582.7 100.2 %collective-permute-start.15 = (bf16[2,256,768]{2,1,0:T(8,128)(2,1)}, bf16[2,256,768]{2,1,0:T(8,128)(2,1)S(1)}, u32[]{:S(2)}, u32[]{:S(2)}) collective-permute-start(bf16[2,256,768]{2,1,0:T(8,128)(2,1)} %convolution_convert_fusion.1), channel_id=1, source_target_pairs={{0,2},{1,3},{2,4},{3,5},{4,6},{5,7},{8,10},{9,11},{10,12},{11,13},... | collective-permute-start | bytes 2359304 | tf_op jit(solution)/shard_map/ppermute | solution.py:17
  642.3 45.8 %collective-permute-start.16 = (bf16[2,256,768]{2,1,0:T(8,128)(2,1)}, bf16[2,256,768]{2,1,0:T(8,128)(2,1)S(1)}, u32[]{:S(2)}, u32[]{:S(2)}) collective-permute-start(bf16[2,256,768]{2,1,0:T(8,128)(2,1)} %convolution_convert_fusion.1), channel_id=1, source_target_pairs={{0,1},{1,2},{2,3},{3,4},{4,5},{5,6},{6,7},{8,9},{9,10},{10,11},{11... | collective-permute-start | bytes 2359304 | tf_op jit(solution)/shard_map/ppermute | solution.py:17
  671.2 71.6 %collective-permute-start.3 = (bf16[2,256,768]{1,2,0:T(8,128)(2,1)}, bf16[2,256,768]{1,2,0:T(8,128)(2,1)S(1)}, u32[]{:S(2)}, u32[]{:S(2)}) collective-permute-start(bf16[2,256,768]{1,2,0:T(8,128)(2,1)} %copy.136), channel_id=1, source_target_pairs={{0,6},{1,7},{8,14},{9,15},{16,22},{17,23},{24,30},{25,31}} | collective-permute-start | bytes 2359304 | tf_op jit(solution)/shard_map/ppermute | solution.py:17
  674.6 89.7 %collective-permute-start.1 = (bf16[2,256,768]{1,2,0:T(8,128)(2,1)}, bf16[2,256,768]{1,2,0:T(8,128)(2,1)S(1)}, u32[]{:S(2)}, u32[]{:S(2)}) collective-permute-start(bf16[2,256,768]{1,2,0:T(8,128)(2,1)} %copy.136), channel_id=1, source_target_pairs={} | collective-permute-start | bytes 2359304 | tf_op jit(solution)/shard_map/ppermute | solution.py:17
  677.3 88.3 %collective-permute-start.2 = (bf16[2,256,768]{1,2,0:T(8,128)(2,1)}, bf16[2,256,768]{1,2,0:T(8,128)(2,1)S(1)}, u32[]{:S(2)}, u32[]{:S(2)}) collective-permute-start(bf16[2,256,768]{1,2,0:T(8,128)(2,1)} %copy.136), channel_id=1, source_target_pairs={{0,7},{8,15},{16,23},{24,31}} | collective-permute-start | bytes 2359304 | tf_op jit(solution)/shard_map/ppermute | solution.py:17
  682.8 85.5 %collective-permute-start.4 = (bf16[2,256,768]{1,2,0:T(8,128)(2,1)}, bf16[2,256,768]{1,2,0:T(8,128)(2,1)}, u32[]{:S(2)}, u32[]{:S(2)}) collective-permute-start(bf16[2,256,768]{1,2,0:T(8,128)(2,1)} %copy.136), channel_id=1, source_target_pairs={{0,5},{1,6},{2,7},{8,13},{9,14},{10,15},{16,21},{17,22},{18,23},{2... | collective-permute-start | bytes 2359304 | tf_op jit(solution)/shard_map/ppermute | solution.py:17
  688.2 81.4 %collective-permute-start.5 = (bf16[2,256,768]{1,2,0:T(8,128)(2,1)}, bf16[2,256,768]{1,2,0:T(8,128)(2,1)}, u32[]{:S(2)}, u32[]{:S(2)}) collective-permute-start(bf16[2,256,768]{1,2,0:T(8,128)(2,1)} %copy.136), channel_id=1, source_target_pairs={{0,4},{1,5},{2,6},{3,7},{8,12},{9,13},{10,14},{11,15},{16,20},{17,... | collective-permute-start | bytes 2359304 | tf_op jit(solution)/shard_map/ppermute | solution.py:17
  742.7 33.4 %collective-permute-start.6 = (bf16[2,256,768]{1,2,0:T(8,128)(2,1)}, bf16[2,256,768]{1,2,0:T(8,128)(2,1)}, u32[]{:S(2)}, u32[]{:S(2)}) collective-permute-start(bf16[2,256,768]{1,2,0:T(8,128)(2,1)} %copy.136), channel_id=1, source_target_pairs={{0,3},{1,4},{2,5},{3,6},{4,7},{8,11},{9,12},{10,13},{11,14},{12,15... | collective-permute-start | bytes 2359304 | tf_op jit(solution)/shard_map/ppermute | solution.py:17
  764.2 26.9 collective-permute-start.7
  765.7 25.6 collective-permute-start.8
  998.8 1868.9 %reduce-scatter.10.cloned.1.call-start = ((), (), s32[]{:S(2)}) async-start(), calls=%async_computation.13 | async-start | bytes 2949120 | tf_op jit(solution)/shard_map/reduce_scatter | solution.py:333
  999.8 601.9 %copy-start.44 = (f32[768]{0:T(1024)S(1)}, f32[768]{0:T(1024)}, u32[]{:S(2)}) copy-start(f32[768]{0:T(1024)} %copy-done.43) | copy-start | bytes 9220
  999.8 601.9 %copy-start.46 = (f32[2,256]{1,0:T(2,128)S(1)}, f32[2,256]{1,0:T(2,128)}, u32[]{:S(2)}) copy-start(f32[2,256]{1,0:T(2,128)} %copy-done.45) | copy-start | bytes 6148
  999.8 601.9 %copy-start.50 = (f32[2,256]{1,0:T(2,128)S(1)}, f32[2,256]{1,0:T(2,128)}, u32[]{:S(2)}) copy-start(f32[2,256]{1,0:T(2,128)} %copy-done.49) | copy-start | bytes 6148
  999.8 601.9 %copy-start.77 = (f32[768]{0:T(1024)S(1)}, f32[768]{0:T(1024)}, u32[]{:S(2)}) copy-start(f32[768]{0:T(1024)} %copy-done.76) | copy-start | bytes 9220
  1605.6 1262.1 %reduce-scatter.14.cloned.1.call-start = ((), (), s32[]{:S(2)}) async-start(), calls=%async_computation.15 | async-start | bytes 2949120 | tf_op jit(solution)/shard_map/reduce_scatter | solution.py:335
  1617.3 52.5 %collective-permute-start.26 = (bf16[2,256,768]{1,2,0:T(8,128)(2,1)S(1)}, bf16[2,256,768]{1,2,0:T(8,128)(2,1)S(1)}, u32[]{:S(2)}, u32[]{:S(2)}) collective-permute-start(bf16[2,256,768]{1,2,0:T(8,128)(2,1)S(1)} %get-tuple-element.676), channel_id=1, source_target_pairs={{1,0},{2,1},{3,2},{4,3},{5,4},{6,5},{7,6},{9,8},{10,9},{11,10},{12... | collective-permute-start | bytes 2359304 | tf_op jit(solution)/shard_map/ppermute | solution.py:17
  1618.6 52.5 %collective-permute-start.33 = (bf16[2,256,768]{1,2,0:T(8,128)(2,1)S(1)}, bf16[2,256,768]{1,2,0:T(8,128)(2,1)S(1)}, u32[]{:S(2)}, u32[]{:S(2)}) collective-permute-start(bf16[2,256,768]{1,2,0:T(8,128)(2,1)S(1)} %get-tuple-element.677), channel_id=1, source_target_pairs={} | collective-permute-start | bytes 2359304 | tf_op jit(solution)/shard_map/ppermute | solution.py:17
  1619.3 53.1 %collective-permute-start.32 = (bf16[2,256,768]{1,2,0:T(8,128)(2,1)S(1)}, bf16[2,256,768]{1,2,0:T(8,128)(2,1)S(1)}, u32[]{:S(2)}, u32[]{:S(2)}) collective-permute-start(bf16[2,256,768]{1,2,0:T(8,128)(2,1)S(1)} %get-tuple-element.678), channel_id=1, source_target_pairs={{7,0},{15,8},{23,16},{31,24}} | collective-permute-start | bytes 2359304 | tf_op jit(solution)/shard_map/ppermute | solution.py:17
  1621.3 81.0 %collective-permute-start.17 = (bf16[2,256,768]{1,2,0:T(8,128)(2,1)S(1)}, bf16[2,256,768]{1,2,0:T(8,128)(2,1)S(1)}, u32[]{:S(2)}, u32[]{:S(2)}) collective-permute-start(bf16[2,256,768]{1,2,0:T(8,128)(2,1)S(1)} %get-tuple-element.684), channel_id=1, source_target_pairs={{1,0},{2,1},{3,2},{4,3},{5,4},{6,5},{7,6},{9,8},{10,9},{11,10},{12... | collective-permute-start | bytes 2359304 | tf_op jit(solution)/shard_map/ppermute | solution.py:17
  1622.6 81.0 %collective-permute-start.24 = (bf16[2,256,768]{1,2,0:T(8,128)(2,1)S(1)}, bf16[2,256,768]{1,2,0:T(8,128)(2,1)S(1)}, u32[]{:S(2)}, u32[]{:S(2)}) collective-permute-start(bf16[2,256,768]{1,2,0:T(8,128)(2,1)S(1)} %get-tuple-element.685), channel_id=1, source_target_pairs={} | collective-permute-start | bytes 2359304 | tf_op jit(solution)/shard_map/ppermute | solution.py:17
  1669.8 35.0 %collective-permute-start.23 = (bf16[2,256,768]{1,2,0:T(8,128)(2,1)S(1)}, bf16[2,256,768]{1,2,0:T(8,128)(2,1)S(1)}, u32[]{:S(2)}, u32[]{:S(2)}) collective-permute-start(bf16[2,256,768]{1,2,0:T(8,128)(2,1)S(1)} %get-tuple-element.686), channel_id=1, source_target_pairs={{7,0},{15,8},{23,16},{31,24}} | collective-permute-start | bytes 2359304 | tf_op jit(solution)/shard_map/ppermute | solution.py:17
  1671.1 117.5 %copy-start.21 = (bf16[2,256,768]{1,2,0:T(8,128)(2,1)}, bf16[2,256,768]{1,2,0:T(8,128)(2,1)S(1)}, u32[]{:S(2)}) copy-start(bf16[2,256,768]{1,2,0:T(8,128)(2,1)S(1)} %collective-permute-done.33) | copy-start | bytes 2359300
  1671.1 36.3 %collective-permute-start.22 = (bf16[2,256,768]{1,2,0:T(8,128)(2,1)S(1)}, bf16[2,256,768]{1,2,0:T(8,128)(2,1)S(1)}, u32[]{:S(2)}, u32[]{:S(2)}) collective-permute-start(bf16[2,256,768]{1,2,0:T(8,128)(2,1)S(1)} %get-tuple-element.687), channel_id=1, source_target_pairs={{6,0},{7,1},{14,8},{15,9},{22,16},{23,17},{30,24},{31,25}} | collective-permute-start | bytes 2359304 | tf_op jit(solution)/shard_map/ppermute | solution.py:17
  1672.5 116.2 %copy-start.22 = (bf16[2,256,768]{1,2,0:T(8,128)(2,1)}, bf16[2,256,768]{1,2,0:T(8,128)(2,1)S(1)}, u32[]{:S(2)}) copy-start(bf16[2,256,768]{1,2,0:T(8,128)(2,1)S(1)} %collective-permute-done.32) | copy-start | bytes 2359300
  1672.5 69.4 %collective-permute-start.21 = (bf16[2,256,768]{1,2,0:T(8,128)(2,1)S(1)}, bf16[2,256,768]{1,2,0:T(8,128)(2,1)S(1)}, u32[]{:S(2)}, u32[]{:S(2)}) collective-permute-start(bf16[2,256,768]{1,2,0:T(8,128)(2,1)S(1)} %get-tuple-element.688), channel_id=1, source_target_pairs={{5,0},{6,1},{7,2},{13,8},{14,9},{15,10},{21,16},{22,17},{23,18},{2... | collective-permute-start | bytes 2359304 | tf_op jit(solution)/shard_map/ppermute | solution.py:17
  1702.2 86.4 %copy-start.23 = (bf16[2,256,768]{1,2,0:T(8,128)(2,1)}, bf16[2,256,768]{1,2,0:T(8,128)(2,1)S(1)}, u32[]{:S(2)}) copy-start(bf16[2,256,768]{1,2,0:T(8,128)(2,1)S(1)} %collective-permute-done.17) | copy-start | bytes 2359300
  1702.2 83.8 %collective-permute-start.20 = (bf16[2,256,768]{1,2,0:T(8,128)(2,1)S(1)}, bf16[2,256,768]{1,2,0:T(8,128)(2,1)S(1)}, u32[]{:S(2)}, u32[]{:S(2)}) collective-permute-start(bf16[2,256,768]{1,2,0:T(8,128)(2,1)S(1)} %get-tuple-element.689), channel_id=1, source_target_pairs={{4,0},{5,1},{6,2},{7,3},{12,8},{13,9},{14,10},{15,11},{20,16},{21,... | collective-permute-start | bytes 2359304 | tf_op jit(solution)/shard_map/ppermute | solution.py:17
  1703.5 85.2 %copy-start.24 = (bf16[2,256,768]{1,2,0:T(8,128)(2,1)}, bf16[2,256,768]{1,2,0:T(8,128)(2,1)S(1)}, u32[]{:S(2)}) copy-start(bf16[2,256,768]{1,2,0:T(8,128)(2,1)S(1)} %collective-permute-done.24) | copy-start | bytes 2359300
  1703.5 83.8 %collective-permute-start.19 = (bf16[2,256,768]{1,2,0:T(8,128)(2,1)S(1)}, bf16[2,256,768]{1,2,0:T(8,128)(2,1)S(1)}, u32[]{:S(2)}, u32[]{:S(2)}) collective-permute-start(bf16[2,256,768]{1,2,0:T(8,128)(2,1)S(1)} %get-tuple-element.690), channel_id=1, source_target_pairs={{3,0},{4,1},{5,2},{6,3},{7,4},{11,8},{12,9},{13,10},{14,11},{15,12... | collective-permute-start | bytes 2359304 | tf_op jit(solution)/shard_map/ppermute | solution.py:17
  1704.8 83.8 %copy-start.25 = (bf16[2,256,768]{1,2,0:T(8,128)(2,1)}, bf16[2,256,768]{1,2,0:T(8,128)(2,1)S(1)}, u32[]{:S(2)}) copy-start(bf16[2,256,768]{1,2,0:T(8,128)(2,1)S(1)} %collective-permute-done.23) | copy-start | bytes 2359300
  1704.9 83.8 %collective-permute-start.18 = (bf16[2,256,768]{1,2,0:T(8,128)(2,1)S(1)}, bf16[2,256,768]{1,2,0:T(8,128)(2,1)S(1)}, u32[]{:S(2)}, u32[]{:S(2)}) collective-permute-start(bf16[2,256,768]{1,2,0:T(8,128)(2,1)S(1)} %get-tuple-element.691), channel_id=1, source_target_pairs={{2,0},{3,1},{4,2},{5,3},{6,4},{7,5},{10,8},{11,9},{12,10},{13,11},... | collective-permute-start | bytes 2359304 | tf_op jit(solution)/shard_map/ppermute | solution.py:17
  1707.4 81.3 %copy-start.26 = (bf16[2,256,768]{1,2,0:T(8,128)(2,1)}, bf16[2,256,768]{1,2,0:T(8,128)(2,1)S(1)}, u32[]{:S(2)}) copy-start(bf16[2,256,768]{1,2,0:T(8,128)(2,1)S(1)} %collective-permute-done.22) | copy-start | bytes 2359300
  1707.4 101.9 %collective-permute-start.31 = (bf16[2,256,768]{1,2,0:T(8,128)(2,1)}, bf16[2,256,768]{1,2,0:T(8,128)(2,1)}, u32[]{:S(2)}, u32[]{:S(2)}) collective-permute-start(bf16[2,256,768]{1,2,0:T(8,128)(2,1)} %get-tuple-element.679), channel_id=1, source_target_pairs={{6,0},{7,1},{14,8},{15,9},{22,16},{23,17},{30,24},{31,25}} | collective-permute-start | bytes 2359304 | tf_op jit(solution)/shard_map/ppermute | solution.py:17
  1741.9 135.1 %collective-permute-start.30 = (bf16[2,256,768]{1,2,0:T(8,128)(2,1)}, bf16[2,256,768]{1,2,0:T(8,128)(2,1)}, u32[]{:S(2)}, u32[]{:S(2)}) collective-permute-start(bf16[2,256,768]{1,2,0:T(8,128)(2,1)} %get-tuple-element.680), channel_id=1, source_target_pairs={{5,0},{6,1},{7,2},{13,8},{14,9},{15,10},{21,16},{22,17},{23,18},{2... | collective-permute-start | bytes 2359304 | tf_op jit(solution)/shard_map/ppermute | solution.py:17
  1786.0 118.2 %collective-permute-start.29 = (bf16[2,256,768]{1,2,0:T(8,128)(2,1)}, bf16[2,256,768]{1,2,0:T(8,128)(2,1)}, u32[]{:S(2)}, u32[]{:S(2)}) collective-permute-start(bf16[2,256,768]{1,2,0:T(8,128)(2,1)} %get-tuple-element.681), channel_id=1, source_target_pairs={{4,0},{5,1},{6,2},{7,3},{12,8},{13,9},{14,10},{15,11},{20,16},{21,... | collective-permute-start | bytes 2359304 | tf_op jit(solution)/shard_map/ppermute | solution.py:17
  1787.3 116.9 %collective-permute-start.28 = (bf16[2,256,768]{1,2,0:T(8,128)(2,1)}, bf16[2,256,768]{1,2,0:T(8,128)(2,1)}, u32[]{:S(2)}, u32[]{:S(2)}) collective-permute-start(bf16[2,256,768]{1,2,0:T(8,128)(2,1)} %get-tuple-element.682), channel_id=1, source_target_pairs={{3,0},{4,1},{5,2},{6,3},{7,4},{11,8},{12,9},{13,10},{14,11},{15,12... | collective-permute-start | bytes 2359304 | tf_op jit(solution)/shard_map/ppermute | solution.py:17
  1789.5 146.6 %collective-permute-start.27 = (bf16[2,256,768]{1,2,0:T(8,128)(2,1)S(1)}, bf16[2,256,768]{1,2,0:T(8,128)(2,1)}, u32[]{:S(2)}, u32[]{:S(2)}) collective-permute-start(bf16[2,256,768]{1,2,0:T(8,128)(2,1)S(1)} %get-tuple-element.683), channel_id=1, source_target_pairs={{2,0},{3,1},{4,2},{5,3},{6,4},{7,5},{10,8},{11,9},{12,10},{13,11},... | collective-permute-start | bytes 2359304 | tf_op jit(solution)/shard_map/ppermute | solution.py:17
  1943.5 931.3 %reduce-scatter.12.cloned.1.call-start = ((), (), s32[]{:S(2)}) async-start(), calls=%async_computation.14 | async-start | bytes 2949120 | tf_op jit(solution)/shard_map/reduce_scatter | solution.py:334
  2832.0 8.7 collective-permute-start.25
  2845.6 110.3 %reduce-scatter.20.cloned.1.call-start = ((), (), s32[]{:S(2)}) async-start(), calls=%async_computation.18 | async-start | bytes 11796480 | tf_op jit(solution)/shard_map/reduce_scatter | solution.py:345
  2856.8 180.0 %reduce-scatter.18.cloned.1.call-start = ((), (), s32[]{:S(2)}) async-start(), calls=%async_computation.17 | async-start | bytes 11796480 | tf_op jit(solution)/shard_map/reduce_scatter | solution.py:344
  2865.6 220.0 %reduce-scatter.22.cloned.1.call-start = ((), (), s32[]{:S(2)}) async-start(), calls=%async_computation.19 | async-start | bytes 491520
  2867.5 437.5 %all-reduce.27.cloned.1.call-start = ((), (), s32[]{:S(2)}) async-start(), calls=%async_computation.20 | async-start | bytes 14155776 | tf_op jit(solution)/shard_map/psum | solution.py:347
  (124 other events, 1021.8 us)
Sparse Core Ops, SparseCore 0:
  9.6 20.2 all-gather.13
  31.5 17.7 all-gather.11
  50.8 17.8 all-gather.9
  70.1 17.8 all-gather.15
  89.4 37.4 all-gather.17
  128.3 37.4 all-gather.19
  998.9 74.0 reduce-scatter.15
  1605.7 73.5 reduce-scatter.9
  1943.6 29.4 reduce-scatter.13
  2845.7 29.0 reduce-scatter.11
  2877.4 78.4 reduce-scatter.19
  2958.3 78.4 reduce-scatter.17
  3039.8 20.8 reduce-scatter.21
  3065.6 239.2 all-reduce.26
where the time goes:
time: 3360 us; the launch traced here: 3320 us
  local copies, waits for them, and re-layouts  1150 us (34%)
  waiting for transfers between devices  670 us (20%)
  other arithmetic  432 us (13%)
  loops' own time  426 us (13%)
  matrix products  346 us (10%)
  starting transfers between devices  195 us (6%)
  blocking collectives  83 us (2%)
    ppermute x34, waiting for transfers between devices, passed_along(): lax.ppermute(value, axis, [(source, source + steps) for source in range(l...  320 us
    dynamic_update_slice x64, local copies, waits for them, and re-layouts, one_tap(): lax.dynamic_update_slice_in_dim(ext_grad, current + masked * weight, firs...  301 us
    another operation x1, loops' own time, shift_backward(): lax.scan(one_tap, jnp.zeros_like(key_ext), jnp.arange(SHIFT))  208 us
    another operation x1, loops' own time, shift_forward(): running, _ = lax.scan(one_tap, start_sum, jnp.arange(SHIFT))  208 us
    ppermute x34, starting transfers between devices, passed_along(): lax.ppermute(value, axis, [(source, source + steps) for source in range(l...  194 us
    add x64, other arithmetic, one_tap(): running + jnp.where(same_doc[..., None], shifted_part, 0.0) * weight  186 us
    psum x1, waiting for transfers between devices, shards(): lax.psum((owned[0], owned[1], owned[2], owned[3], owned[4], owned[5], own...  177 us
    reduce_sum x64, other arithmetic, one_tap(): tap_grad = jnp.sum(masked * shifted_part, axis=(0, 1))  156 us
  transfers between devices with their start and end apart: 48, of which 17 were waited for; matrix products, arithmetic and copies ran while one was open for 56% of the time, Pallas kernels for 0%

commit v1 on v0

v1 whole, which is shorter than its diff:
```python
import functools

import jax
import jax.numpy as jnp
import numpy as np
from jax import lax
from jax.experimental import pallas as pl
from jax.experimental.pallas import tpu as pltpu
from jax.sharding import PartitionSpec as P

SHIFT = 64
HOPS = 8
TILE = 256
HALO = 64
EPS = 1e-05
BF = jnp.bfloat16
F32 = jnp.float32
VMEM_BYTES = 56 * 1024 * 1024


def vmem():
    return pl.BlockSpec(memory_space=pltpu.VMEM)


def smem():
    return pl.BlockSpec(memory_space=pltpu.SMEM)


def params():
    return pltpu.CompilerParams(vmem_limit_bytes=VMEM_BYTES)


def mm(left, right):
    return lax.dot_general(left, right, (((1,), (0,)), ((), ())), preferred_element_type=F32)


def mm_nt(left, right):
    return lax.dot_general(left, right, (((1,), (1,)), ((), ())), preferred_element_type=F32)


def lane_tiles(width):
    return [(base, min(128, width - base)) for base in range(0, width, 128)]


def fill_ext(ext_ref, first_row, rows, source_ref, width):
    for index, (base, size) in enumerate(lane_tiles(width)):
        if size < 128:
            ext_ref[index, pl.ds(first_row, rows), :] = jnp.zeros((rows, 128), F32)
        ext_ref[index, pl.ds(first_row, rows), 0:size] = source_ref[:, base : base + size].astype(F32)


def shift_fwd_kernel(seg_s, k_ref, halo_ref, taps_ref, segcol_ref, out_ref, ext, seg_b):
    rows, width = k_ref.shape
    fill_ext(ext, 0, HALO, halo_ref, width)
    fill_ext(ext, HALO, rows, k_ref, width)
    seg_b[...] = jnp.broadcast_to(segcol_ref[...], seg_b.shape)
    for index, (base, size) in enumerate(lane_tiles(width)):

        def tap_row(lag):
            return taps_ref[index, lag : lag + 1, :]

        def body(tile, carry):
            start = pl.multiple_of(tile * 64, 64)

            def plain():
                total = jnp.zeros((64, 128), F32)
                for lag in range(SHIFT):
                    total = total + ext[index, pl.ds(start + HALO - lag, 64), :] * tap_row(lag)
                return total

            def masked():
                total = jnp.zeros((64, 128), F32)
                now = seg_b[pl.ds(start + HALO, 64), :]
                for lag in range(SHIFT):
                    same = seg_b[pl.ds(start + HALO - lag, 64), :] == now
                    part = ext[index, pl.ds(start + HALO - lag, 64), :] * tap_row(lag)
                    total = total + jnp.where(same, part, 0.0)
                return total

            total = lax.cond(seg_s[start + 1] == seg_s[start + HALO + 63], plain, masked)
            out_ref[pl.ds(start, 64), base : base + size] = total[:, 0:size].astype(BF)
            return carry

        lax.fori_loop(0, rows // 64, body, 0)


def shift_fwd(seg_full, k_own, k_halo, taps):
    rows, width = k_own.shape
    tiles = len(lane_tiles(width))
    return pl.pallas_call(
        shift_fwd_kernel,
        out_shape=jax.ShapeDtypeStruct((rows, width), BF),
        in_specs=[smem(), vmem(), vmem(), vmem(), vmem()],
        out_specs=vmem(),
        scratch_shapes=[
            pltpu.VMEM((tiles, HALO + rows, 128), F32),
            pltpu.VMEM((HALO + rows, 128), jnp.int32),
        ],
        compiler_params=params(),
        name="shift_fwd",
    )(seg_full, k_own, k_halo, taps, seg_full[: HALO + rows, None])


def shift_bwd_kernel(
    seg_s, k_ref, halo_ref, g_ref, ghalo_ref, taps_ref, segcol_ref, gk_ref, tg_ref, ext, gext, seg_b, acc
):
    rows, width = k_ref.shape
    fill_ext(ext, 0, HALO, halo_ref, width)
    fill_ext(ext, HALO, rows, k_ref, width)
    fill_ext(gext, 0, rows, g_ref, width)
    fill_ext(gext, rows, HALO, ghalo_ref, width)
    seg_b[...] = jnp.broadcast_to(segcol_ref[...], seg_b.shape)
    acc[...] = jnp.zeros_like(acc)
    for index, (base, size) in enumerate(lane_tiles(width)):

        def tap_row(lag):
            return taps_ref[index, lag : lag + 1, :]

        def fold(part):
            total = part[0:8]
            for piece in range(1, 8):
                total = total + part[8 * piece : 8 * piece + 8]
            return total

        def body(tile, carry):
            start = pl.multiple_of(tile * 64, 64)

            def plain():
                total = jnp.zeros((64, 128), F32)
                for lag in range(SHIFT):
                    total = total + gext[index, pl.ds(start + lag, 64), :] * tap_row(lag)
                return total

            def masked():
                total = jnp.zeros((64, 128), F32)
                now = seg_b[pl.ds(start + HALO, 64), :]
                for lag in range(SHIFT):
                    same = seg_b[pl.ds(start + HALO + lag, 64), :] == now
                    part = gext[index, pl.ds(start + lag, 64), :] * tap_row(lag)
                    total = total + jnp.where(same, part, 0.0)
                return total

            total = lax.cond(seg_s[start + HALO] == seg_s[start + HALO + 126], plain, masked)
            gk_ref[pl.ds(start, 64), base : base + size] = total[:, 0:size].astype(BF)
            grad = gext[index, pl.ds(start, 64), :]
            clear = seg_s[start + 1] == seg_s[start + HALO + 63]

            @pl.when(clear)
            def _():
                for lag in range(SHIFT):
                    part = ext[index, pl.ds(start + HALO - lag, 64), :] * grad
                    acc[index, lag] = acc[index, lag] + fold(part)

            @pl.when(jnp.logical_not(clear))
            def _():
                now = seg_b[pl.ds(start + HALO, 64), :]
                for lag in range(SHIFT):
                    same = seg_b[pl.ds(start + HALO - lag, 64), :] == now
                    part = ext[index, pl.ds(start + HALO - lag, 64), :] * grad
                    acc[index, lag] = acc[index, lag] + fold(jnp.where(same, part, 0.0))

            return carry

        lax.fori_loop(0, rows // 64, body, 0)
        tg_ref[:, base : base + size] = jnp.sum(acc[index], axis=1)[:, 0:size]


def shift_bwd(seg_full, k_own, k_halo, grad, grad_halo, taps):
    rows, width = k_own.shape
    tiles = len(lane_tiles(width))
    return pl.pallas_call(
        shift_bwd_kernel,
        out_shape=(jax.ShapeDtypeStruct((rows, width), BF), jax.ShapeDtypeStruct((SHIFT, width), F32)),
        in_specs=[smem()] + [vmem()] * 6,
        out_specs=(vmem(), vmem()),
        scratch_shapes=[
            pltpu.VMEM((tiles, HALO + rows, 128), F32),
            pltpu.VMEM((tiles, HALO + rows, 128), F32),
            pltpu.VMEM((2 * HALO + rows, 128), jnp.int32),
            pltpu.VMEM((tiles, SHIFT, 8, 128), F32),
        ],
        compiler_params=params(),
        name="shift_bwd",
    )(seg_full, k_own, k_halo, grad, grad_halo, taps, seg_full[:, None])


def tile_table(query_blocks, key_blocks, unroll):
    offset = key_blocks - query_blocks
    pairs = []
    for distance in range(HOPS + 1):
        for row in range(query_blocks):
            if row + offset - distance >= 0:
                pairs.append((row, row + offset - distance))
    assert len(pairs) % unroll == 0
    return np.array(pairs, np.int32)


def build_bands(bands, row):
    length = row.shape[1]
    skewed = pltpu.roll(jnp.broadcast_to(row, (8, length)), 0, 1, stride=1, stride_axis=0)
    for step in range(16):
        bands[step] = pltpu.roll(skewed, 8 * step, 1) if step else skewed


def read_band(bands, first, second):
    upper = bands[:, :, pl.ds(first, TILE)].reshape(128, TILE)
    lower = bands[:, :, pl.ds(second, TILE)].reshape(128, TILE)
    return jnp.concatenate([upper, lower], axis=0)


def split_heads(dest, source, heads, size):
    for head in range(heads):
        dest[head] = source[:, head * size : (head + 1) * size]


UNROLL_F = 4
UNROLL_B = 2


def mix_fwd_kernel(tab, q_ref, k_ref, v_ref, row_ref, segq_ref, segk_ref, y_ref, qh, kh, vh, yacc, bands, seg_b):
    heads, length = row_ref.shape[0], row_ref.shape[2]
    size = q_ref.shape[1] // heads
    offset = (k_ref.shape[0] - q_ref.shape[0]) // TILE
    tiles = tab.shape[0]
    split_heads(qh, q_ref, heads, size)
    split_heads(kh, k_ref, heads, size)
    split_heads(vh, v_ref, heads, size)
    seg_b[...] = jnp.broadcast_to(segq_ref[...], seg_b.shape)
    yacc[...] = jnp.zeros_like(yacc)

    def head_body(head, carry):
        build_bands(bands, row_ref[head])

        def body(step, carry):
            for unrolled in range(UNROLL_F):
                row = tab[step * UNROLL_F + unrolled, 0]
                col = tab[step * UNROLL_F + unrolled, 1]
                rows = pl.ds(pl.multiple_of(row * TILE, TILE), TILE)
                cols = pl.ds(pl.multiple_of(col * TILE, TILE), TILE)
                base = pl.multiple_of((length - TILE) - TILE * (row + offset - col), TILE)
                kern = read_band(bands, base, pl.multiple_of(base - 128, 128))
                score = mm_nt(qh[head, rows, :], kh[head, cols, :])
                seg_now = seg_b[rows, :]
                live = jnp.concatenate([seg_now, seg_now], axis=1) == segk_ref[col]
                weight = jnp.where(live, score * kern, 0.0).astype(BF)
                yacc[head, rows, :] += mm(weight, vh[head, cols, :])
            return carry

        lax.fori_loop(0, tiles // UNROLL_F, body, 0)
        return carry

    lax.fori_loop(0, heads, head_body, 0)
    for head in range(heads):
        y_ref[:, head * size : (head + 1) * size] = yacc[head].astype(BF)


def mix_fwd(q, k_win, v_win, kern_desc, seg_q, seg_k):
    rows, width = q.shape
    wide = k_win.shape[0]
    heads, _, length = kern_desc.shape
    size = width // heads
    table = tile_table(rows // TILE, wide // TILE, UNROLL_F)
    return pl.pallas_call(
        mix_fwd_kernel,
        out_shape=jax.ShapeDtypeStruct((rows, width), BF),
        in_specs=[smem()] + [vmem()] * 6,
        out_specs=vmem(),
        scratch_shapes=[
            pltpu.VMEM((heads, rows, size), BF),
            pltpu.VMEM((heads, wide, size), BF),
            pltpu.VMEM((heads, wide, size), BF),
            pltpu.VMEM((heads, rows, size), F32),
            pltpu.VMEM((16, 8, length), F32),
            pltpu.VMEM((rows, 128), jnp.int32),
        ],
        compiler_params=params(),
        name="mix_fwd",
    )(table, q, k_win, v_win, kern_desc, seg_q[:, None], seg_k.reshape(wide // TILE, 1, TILE))


def mix_bwd_kernel(
    tab, q_ref, k_ref, v_ref, g_ref, row_ref, segq_ref, segk_ref, gq_ref, gk_ref, gv_ref, gkern_ref,
    qh, kh, vh, gh, kt, gqt, gkacc, gvacc, bands, gbands, seg_b,
):
    heads, length = row_ref.shape[0], row_ref.shape[2]
    size = q_ref.shape[1] // heads
    query_blocks, key_blocks = q_ref.shape[0] // TILE, k_ref.shape[0] // TILE
    offset = key_blocks - query_blocks
    tiles = tab.shape[0]
    split_heads(qh, q_ref, heads, size)
    split_heads(kh, k_ref, heads, size)
    split_heads(vh, v_ref, heads, size)
    split_heads(gh, g_ref, heads, size)
    for head in range(heads):
        for block in range(key_blocks):
            kt[head, block] = kh[head, block * TILE : (block + 1) * TILE, :].T
    seg_b[...] = jnp.broadcast_to(segk_ref[...], seg_b.shape)
    gqt[...] = jnp.zeros_like(gqt)
    gkacc[...] = jnp.zeros_like(gkacc)
    gvacc[...] = jnp.zeros_like(gvacc)

    def head_body(head, carry):
        build_bands(bands, row_ref[head])
        gbands[...] = jnp.zeros_like(gbands)

        def body(step, carry):
            for unrolled in range(UNROLL_B):
                row = tab[step * UNROLL_B + unrolled, 0]
                col = tab[step * UNROLL_B + unrolled, 1]
                rows = pl.ds(pl.multiple_of(row * TILE, TILE), TILE)
                cols = pl.ds(pl.multiple_of(col * TILE, TILE), TILE)
                first = pl.multiple_of(TILE + TILE * (row + offset - col), TILE)
                second = pl.multiple_of(first - 128, 128)
                kern = read_band(bands, first, second)
                q_now, g_now = qh[head, rows, :], gh[head, rows, :]
                score = mm_nt(kh[head, cols, :], q_now)
                grad = mm_nt(vh[head, cols, :], g_now)
                seg_now = seg_b[cols, :]
                live = jnp.concatenate([seg_now, seg_now], axis=1) == segq_ref[row]
                grad = jnp.where(live, grad, 0.0)
                weight = jnp.where(live, score * kern, 0.0).astype(BF)
                gscore = (grad * kern).astype(BF)
                both = grad * score
                gbands[:, :, pl.ds(first, TILE)] += both[0:128].reshape(16, 8, TILE)
                gbands[:, :, pl.ds(second, TILE)] += both[128:256].reshape(16, 8, TILE)
                gkacc[head, cols, :] += mm(gscore, q_now)
                gvacc[head, cols, :] += mm(weight, g_now)
                gqt[head, row] += mm(kt[head, col], gscore)
            return carry

        lax.fori_loop(0, tiles // UNROLL_B, body, 0)
        total = gbands[0]
        for step in range(1, 16):
            total = total + pltpu.roll(gbands[step], length - 8 * step, 1)
        line = total[0:1]
        for sub in range(1, 8):
            line = line + pltpu.roll(total, length - sub, 1)[sub : sub + 1]
        gkern_ref[head] = line
        return carry

    lax.fori_loop(0, heads, head_body, 0)
    for head in range(heads):
        lanes = slice(head * size, (head + 1) * size)
        for block in range(query_blocks):
            gq_ref[block * TILE : (block + 1) * TILE, lanes] = gqt[head, block].T.astype(BF)
        gk_ref[:, lanes] = gkacc[head]
        gv_ref[:, lanes] = gvacc[head].astype(gv_ref.dtype)


def mix_bwd(q, k_win, v_win, grad, kern_asc, seg_q, seg_k):
    rows, width = q.shape
    wide = k_win.shape[0]
    heads, _, length = kern_asc.shape
    size = width // heads
    table = tile_table(rows // TILE, wide // TILE, UNROLL_B)
    return pl.pallas_call(
        mix_bwd_kernel,
        out_shape=(
            jax.ShapeDtypeStruct((rows, width), BF),
            jax.ShapeDtypeStruct((wide, width), F32),
            jax.ShapeDtypeStruct((wide, width), BF if wide == rows else F32),
            jax.ShapeDtypeStruct((heads, 1, length), F32),
        ),
        in_specs=[smem()] + [vmem()] * 7,
        out_specs=(vmem(),) * 4,
        scratch_shapes=[
            pltpu.VMEM((heads, rows, size), BF),
            pltpu.VMEM((heads, wide, size), BF),
            pltpu.VMEM((heads, wide, size), BF),
            pltpu.VMEM((heads, rows, size), BF),
            pltpu.VMEM((heads, wide // TILE, size, TILE), BF),
            pltpu.VMEM((heads, rows // TILE, size, TILE), F32),
            pltpu.VMEM((heads, wide, size), F32),
            pltpu.VMEM((heads, wide, size), F32),
            pltpu.VMEM((16, 8, length), F32),
            pltpu.VMEM((16, 8, length), F32),
            pltpu.VMEM((wide, 128), jnp.int32),
        ],
        compiler_params=params(),
        name="mix_bwd",
    )(table, q, k_win, v_win, grad, kern_asc, seg_q.reshape(rows // TILE, 1, TILE), seg_k[:, None])


def xor_permute(value, axis, mask):
    count = lax.axis_size(axis)
    return lax.ppermute(value, axis, [(source, source ^ mask) for source in range(count)])


def gather_fsdp(shard):
    me = lax.axis_index("fsdp")
    across = xor_permute(shard, "fsdp", 2)
    beside = xor_permute(shard, "fsdp", 1)
    both = xor_permute(across, "fsdp", 1)
    full = jnp.zeros((4,) + shard.shape, shard.dtype)
    zero = (0,) * shard.ndim
    for mask, part in ((0, shard), (1, beside), (2, across), (3, both)):
        full = lax.dynamic_update_slice(full, part[None], (me ^ mask,) + zero)
    return full


def reduce_grad(partial, groups):
    me = lax.axis_index("fsdp")
    high, low = me // 2, me % 2
    rows, cols = partial.shape[1:]
    pairs = partial.reshape(2, 2, rows, cols)
    keep = lax.dynamic_index_in_dim(pairs, low, 1, keepdims=False)
    send = lax.dynamic_index_in_dim(pairs, 1 - low, 1, keepdims=False).astype(BF)
    total = keep + xor_permute(send, "fsdp", 1).astype(F32)
    keep = lax.dynamic_index_in_dim(total, high, 0, keepdims=False)
    send = lax.dynamic_index_in_dim(total, 1 - high, 0, keepdims=False).astype(BF)
    total = keep + xor_permute(send, "fsdp", 2).astype(F32)
    count = lax.axis_size("dp")
    split = total.astype(BF).reshape(count, rows // count, cols)
    owned = jnp.sum(lax.all_to_all(split, "dp", 0, 0).astype(F32), axis=0).astype(BF)
    spread = jnp.broadcast_to(owned[None], (count,) + owned.shape)
    return lax.all_to_all(spread, "dp", 0, 0).reshape(rows, cols).astype(F32)


def layer_norm(inputs, scales, offsets):
    row_mean = jnp.mean(inputs, axis=-1, keepdims=True)
    centered = inputs - row_mean
    spread = jnp.mean(centered * centered, axis=-1, keepdims=True)
    return centered * lax.rsqrt(spread + EPS) * scales + offsets


def kernel_rows(rate, freq, coef, skip, lags, reach):
    lag = lags.astype(F32)
    inside = (lags >= 0) & (lags < reach)
    clipped = jnp.where(inside, lag, 0.0)
    decay = jnp.exp(-rate[:, :, None] * clipped)
    angle = freq[:, :, None] * clipped
    wave = coef[0][:, :, None] * jnp.cos(angle) - coef[1][:, :, None] * jnp.sin(angle)
    first = (lags == 0).astype(F32)
    return jnp.where(inside, jnp.sum(decay * wave, axis=1) + skip[:, None] * first, 0.0)


def shards(
    tokens, segments, ln1_gain, ln1_bias, w_query, w_key, w_value, shift_taps, ssm_rate, ssm_freq,
    ssm_coef, ssm_skip, w_out, ln2_gain, ln2_bias, w_up, w_down, cotangent,
):
    seqs, rows, width = tokens.shape
    fsdp = lax.axis_size("fsdp")
    dp = lax.axis_size("dp")
    run = HOPS
    assert dp % run == 0 and rows == TILE and fsdp == 4
    me = lax.axis_index("dp")
    chunk, inner = me // run, me % run
    group_count = run // seqs
    share = width // group_count
    seq, group = inner // group_count, inner % group_count
    span = run * rows
    multi = dp > run
    groups = [list(range(base, base + run)) for base in range(0, dp, run)] if multi else None
    reach = HOPS * rows + rows

    def exchange(value):
        return lax.all_to_all(value, "dp", 0, 0, axis_index_groups=groups)

    def to_runs(value):
        split = value.reshape(seqs, rows, group_count, share).transpose(0, 2, 1, 3)
        return exchange(split.reshape(run, rows, share)).reshape(span, share)

    def from_runs(value):
        back = exchange(value.reshape(run, rows, share)).reshape(seqs, group_count, rows, share)
        return back.transpose(0, 2, 1, 3).reshape(seqs * rows, width)

    def from_prev(value):
        if not multi:
            return jnp.zeros_like(value)
        return lax.ppermute(value, "dp", [(src, src + run) for src in range(dp - run)])

    def from_next(value):
        if not multi:
            return jnp.zeros_like(value)
        return lax.ppermute(value, "dp", [(src + run, src) for src in range(dp - run)])

    small_parts = (ln1_gain, ln1_bias, shift_taps, ssm_rate, ssm_freq, ssm_coef, ssm_skip, ln2_gain, ln2_bias)
    flat = jnp.concatenate([part.reshape(-1) for part in small_parts])
    padded = -(-flat.shape[0] // 1024) * 1024
    flat = jnp.pad(flat, (0, padded - flat.shape[0])).reshape(padded // 128, 128)
    small = gather_fsdp(flat).reshape(fsdp, padded)
    pieces, at = [], 0
    for part in small_parts:
        pieces.append(small[:, at : at + part.size])
        at += part.size
    gain_one, bias_one, gain_two, bias_two = (
        pieces[index].reshape(width).astype(F32) for index in (0, 1, 7, 8)
    )

    def mine(piece, shape):
        return lax.dynamic_index_in_dim(piece, group, 0, keepdims=False).reshape(shape).astype(F32)

    heads = ssm_rate.shape[0]
    taps = mine(pieces[2], shift_taps.shape)
    rate = mine(pieces[3], ssm_rate.shape)
    freq = mine(pieces[4], ssm_freq.shape)
    coef = mine(pieces[5], ssm_coef.shape)
    skip = mine(pieces[6], ssm_skip.shape)
    assert fsdp == group_count
    query_w = gather_fsdp(w_query).reshape(width, width)
    key_w = gather_fsdp(w_key).reshape(width, width)
    value_w = gather_fsdp(w_value).reshape(width, width)
    out_w = gather_fsdp(w_out).reshape(width, width)
    up_w = gather_fsdp(w_up).reshape(width, -1)
    down_w = gather_fsdp(w_down).reshape(-1, width)
    hidden_size = up_w.shape[1]

    length = reach + TILE
    lag_up = jnp.arange(length) - TILE
    lag_down = reach - jnp.arange(length)
    kern_asc, kern_pull = jax.vjp(
        lambda *leaves: kernel_rows(*leaves, lag_up, reach), rate, freq, coef, skip
    )
    kern_desc = kernel_rows(rate, freq, coef, skip, lag_down, reach)

    seg_row = lax.dynamic_index_in_dim(segments, seq, 0, keepdims=False)
    seg_wide = jnp.concatenate(
        [jnp.full((span,), -1, jnp.int32), seg_row, jnp.full((HALO,), -2, jnp.int32)]
    )
    seg_full = lax.dynamic_slice_in_dim(seg_wide, chunk * span + span - HALO, span + 2 * HALO, 0)
    seg_q = seg_full[HALO : HALO + span]
    seg_k = lax.dynamic_slice_in_dim(seg_wide, chunk * span, 2 * span, 0) if multi else seg_q

    taps_tiles = jnp.pad(taps, ((0, 0), (0, -share % 128)))
    taps_tiles = taps_tiles.reshape(SHIFT, -1, 128).transpose(1, 0, 2)

    inputs = tokens.reshape(seqs * rows, width).astype(F32)
    normed, norm_one_pull = jax.vjp(layer_norm, inputs, gain_one, bias_one)
    act_one = normed.astype(BF)
    k_own = to_runs(mm(act_one, key_w).astype(BF))
    q_own = to_runs(mm(act_one, query_w).astype(BF))
    v_own = to_runs(mm(act_one, value_w).astype(BF))
    k_halo = from_prev(k_own[span - HALO :])
    ks_own = shift_fwd(seg_full, k_own, k_halo, taps_tiles)
    if multi:
        ks_win = jnp.concatenate([from_prev(ks_own), ks_own], axis=0)
        v_win = jnp.concatenate([from_prev(v_own), v_own], axis=0)
    else:
        ks_win, v_win = ks_own, v_own
    y_own = mix_fwd(q_own, ks_win, v_win, kern_desc[:, None, :], seg_q, seg_k)
    mixed = from_runs(y_own)
    resid = inputs + mm(mixed, out_w)
    normed_two, norm_two_pull = jax.vjp(layer_norm, resid, gain_two, bias_two)
    act_two = normed_two.astype(BF)
    gelu_rows, gelu_pull = jax.vjp(lambda entries: jax.nn.gelu(entries, approximate=True), mm(act_two, up_w))
    hidden = gelu_rows.astype(BF)
    output = (resid + mm(hidden, down_w)).astype(BF)

    def tn(left, right):
        return lax.dot_general(left, right, (((0,), (0,)), ((), ())), preferred_element_type=F32)

    cot = cotangent.reshape(seqs * rows, width)
    down_grad = tn(hidden, cot)
    up_grad_rows = gelu_pull(mm_nt(cot, down_w))[0].astype(BF)
    up_grad = tn(act_two, up_grad_rows)
    resid_part, gain_two_grad, bias_two_grad = norm_two_pull(mm_nt(up_grad_rows, up_w))
    resid_grad = cot.astype(F32) + resid_part
    resid_low = resid_grad.astype(BF)
    out_grad = tn(mixed, resid_low)
    gy_own = to_runs(mm_nt(resid_low, out_w).astype(BF))
    gq_own, gks_win, gv_win, gkern = mix_bwd(
        q_own, ks_win, v_win, gy_own, kern_asc[:, None, :], seg_q, seg_k
    )
    if multi:
        gks_own = gks_win[span:] + from_next(gks_win[:span].astype(BF)).astype(F32)
        gv_own = (gv_win[span:] + from_next(gv_win[:span].astype(BF)).astype(F32)).astype(BF)
        gks_halo = from_next(gks_own[:HALO].astype(BF)).astype(F32)
    else:
        gks_own, gv_own = gks_win, gv_win
        gks_halo = jnp.zeros((HALO, share), F32)
    gk_own, taps_grad = shift_bwd(seg_full, k_own, k_halo, gks_own, gks_halo, taps_tiles)
    rate_grad, freq_grad, coef_grad, skip_grad = kern_pull(gkern[:, 0, :])
    gq = from_runs(gq_own)
    gv = from_runs(gv_own)
    gk = from_runs(gk_own)
    query_grad, key_grad, value_grad = tn(act_one, gq), tn(act_one, gk), tn(act_one, gv)
    act_one_grad = mm_nt(gq, query_w) + mm_nt(gk, key_w) + mm_nt(gv, value_w)
    input_part, gain_one_grad, bias_one_grad = norm_one_pull(act_one_grad)
    input_grad = (resid_grad + input_part).astype(BF)

    big = [
        reduce_grad(grad.reshape(fsdp, grad.shape[0] // fsdp, grad.shape[1]), groups)
        for grad in (query_grad, key_grad, value_grad, out_grad, up_grad, down_grad)
    ]
    by_shard = jnp.concatenate(
        [
            grad.reshape(fsdp, width // fsdp)
            for grad in (gain_one_grad, bias_one_grad, gain_two_grad, bias_two_grad)
        ],
        axis=1,
    )
    by_group = jnp.concatenate(
        [grad.reshape(-1) for grad in (taps_grad, rate_grad, freq_grad, coef_grad, skip_grad)]
    )
    slots = (jnp.arange(group_count) == group)[:, None]
    packed = jnp.concatenate([by_shard, jnp.where(slots, by_group[None], 0.0)], axis=1)
    summed = lax.psum(packed, ("fsdp", "dp"))
    owned = lax.dynamic_index_in_dim(summed, lax.axis_index("fsdp"), 0, keepdims=False)
    shapes = [ln1_gain.shape, ln1_bias.shape, ln2_gain.shape, ln2_bias.shape, shift_taps.shape]
    shapes += [ssm_rate.shape, ssm_freq.shape, ssm_coef.shape, ssm_skip.shape]
    little, at = [], 0
    for shape in shapes:
        count = int(np.prod(shape))
        little.append(owned[at : at + count].reshape(shape))
        at += count
    return (
        output.reshape(seqs, rows, width),
        input_grad.reshape(seqs, rows, width),
        little[0],
        little[1],
        big[0],
        big[1],
        big[2],
        little[4],
        little[5],
        little[6],
        little[7],
        little[8],
        big[3],
        little[2],
        little[3],
        big[4],
        big[5],
    )


def solution(mesh):
    return jax.shard_map(
        shards,
        mesh=mesh,
        in_specs=(
            P("fsdp", "dp", None),
            P("fsdp", None),
            P("fsdp"),
            P("fsdp"),
            P("fsdp", None),
            P("fsdp", None),
            P("fsdp", None),
            P(None, "fsdp"),
            P("fsdp", None),
            P("fsdp", None),
            P(None, "fsdp", None),
            P("fsdp"),
            P("fsdp", None),
            P("fsdp"),
            P("fsdp"),
            P("fsdp", None),
            P("fsdp", None),
            P("fsdp", "dp", None),
        ),
        out_specs=(
            P("fsdp", "dp", None),
            P("fsdp", "dp", None),
            P("fsdp"),
            P("fsdp"),
            P("fsdp", None),
            P("fsdp", None),
            P("fsdp", None),
            P(None, "fsdp"),
            P("fsdp", None),
            P("fsdp", None),
            P(None, "fsdp", None),
            P("fsdp"),
            P("fsdp", None),
            P("fsdp"),
            P("fsdp"),
            P("fsdp", None),
            P("fsdp", None),
        ),
        check_vma=False,
    )
```

time: 3360 us -> 809 us (0.24)
  local copies, waits for them, and re-layouts: 1150 us -> 149 us
  loops' own time: 426 us -> 0 us
  waiting for transfers between devices: 670 us -> 293 us
  other arithmetic: 432 us -> 59.4 us
  matrix products: 346 us -> 54.2 us
  Pallas kernels: 0 us -> 110 us
  blocking collectives: 83 us -> 0 us
  starting transfers between devices: 195 us -> 116 us
    another operation x4 -> x0, loops' own time: 426 us -> none  [the longest x1 208 us: shift_backward(): lax.scan(one_tap, jnp.zeros_like(key_ext), jnp.arange(SHIFT))]
    dynamic_update_slice x140 -> x27, local copies, waits for them, and re-layouts: 407 us -> 30.7 us  [gather_fsdp(): full = lax.dynamic_update_slice(full, part[None], (me ^ mask,) + zero)]
    dot_general x90 -> x18, matrix products: 346 us -> 54.2 us  [the longest x6 23 us: mm(): lax.dot_general(left, right, (((1,), (0,)), ((), ())), preferred_element_...]
    ppermute x34 -> x33, waiting for transfers between devices: 320 us -> 54.4 us  [xor_permute(): lax.ppermute(value, axis, [(source, source ^ mask) for source in range(co...]
    dynamic_slice x282 -> x2, local copies, waits for them, and re-layouts: 214 us -> 0.78 us  [the longest x1 0.77 us: mine(): lax.dynamic_index_in_dim(piece, group, 0, keepdims=False).reshape(shape)]
    reduce_sum x80 -> x10, other arithmetic: 211 us -> 18.8 us  [the longest x1 8.3 us: kernel_rows(): jnp.sum(decay * wave, axis=1) + skip[:, None] * first]
    add x67 -> x6, other arithmetic: 190 us -> 10.3 us  [reduce_grad(): total = keep + xor_permute(send, 'fsdp', 1).astype(F32)]
    ppermute x34 -> x33, starting transfers between devices: 194 us -> 18.8 us  [xor_permute(): lax.ppermute(value, axis, [(source, source ^ mask) for source in range(co...]
  transfers between devices with their start and end apart: 48 -> 54, of which waited for: 17 -> 17; matrix products, arithmetic and copies ran while one was open for 56% -> 26% of each run, Pallas kernels for 0% -> 14%
where the time goes in v1:
time: 809 us; the launch traced here: 797 us
  waiting for transfers between devices  293 us (36%)
  local copies, waits for them, and re-layouts  149 us (18%)
  starting transfers between devices  116 us (14%)
  Pallas kernels  110 us (14%)
  other arithmetic  59.4 us (7%)
  matrix products  54.2 us (7%)
  between operations  15.9 us (2%)
    psum x1, waiting for transfers between devices, shards(): summed = lax.psum(packed, ('fsdp', 'dp'))  134 us
    ppermute x33, waiting for transfers between devices, xor_permute(): lax.ppermute(value, axis, [(source, source ^ mask) for source in range(co...  54.4 us
    pallas_call x1, Pallas kernels, mix_bwd(): pl.pallas_call(mix_bwd_kernel, out_shape=(jax.ShapeDtypeStruct((rows, wid...  46.5 us
    all_to_all x8, starting transfers between devices, exchange(): return lax.all_to_all(value, 'dp', 0, 0, axis_index_groups=groups)  43.6 us
    all_to_all x6, waiting for transfers between devices, reduce_grad(): return lax.all_to_all(spread, 'dp', 0, 0).reshape(rows, cols).astype(F32)  35.1 us
    all_to_all x8, waiting for transfers between devices, exchange(): return lax.all_to_all(value, 'dp', 0, 0, axis_index_groups=groups)  35 us
    all_to_all x6, waiting for transfers between devices, reduce_grad(): lax.all_to_all(split, 'dp', 0, 0).astype(F32)  34 us
    dynamic_update_slice x27, local copies, waits for them, and re-layouts, gather_fsdp(): full = lax.dynamic_update_slice(full, part[None], (me ^ mask,) + zero)  30.7 us
  transfers between devices with their start and end apart: 54, of which 17 were waited for; matrix products, arithmetic and copies ran while one was open for 26% of the time, Pallas kernels for 14%

profile of v1, /device:TPU:0, one launch (start us, length us, event | category | flops | bytes accessed | tf_op | source)
XLA Modules:
  0.0 797.1 jit_solution(12524158336945672695)
XLA Ops:
  10.5 3.4 concatenate.12
  15.0 2.5 collective-permute-start.1
  42.1 8.3 %fusion.59 = (f32[3,2560]{1,0:T(4,128)}, f32[3,2560]{1,0:T(4,128)}) fusion(f32[2560]{0:T(1024)S(1)} %copy-done.68, f32[3,32]{1,0:T(4,128)S(1)} %mul.375, f32[3,32]{1,0:T(4,128)S(1)} %reshape.734, f32[3,32]{1,0:T(4,128)S(1)} %mul.370, f32[3,32]{1,0:T(4,128)S(1)} %neg.34, f32[2560]{0:T(1024)S(1)} %copy-done.70), kind=kLoop, calls=%fused_computation.113 | loop fusion | flops 3425280 | bytes 83456 | tf_op jit(solution)/shard_map/jvp()/reduce_sum | solution.py:434
  59.7 6.0 all-to-all-start
  77.6 2.9 convolution_convert_fusion.2
  86.2 5.2 all-to-all-start.1
  106.8 2.9 reshape.689
  112.2 13.2 %collective-permute-done.16 = bf16[192,3072]{1,0:T(8,128)(2,1)} collective-permute-done((bf16[192,3072]{1,0:T(8,128)(2,1)}, bf16[192,3072]{1,0:T(8,128)(2,1)}, u32[]{:S(2)}, u32[]{:S(2)}) %collective-permute-start.16) | collective-permute-done | bytes 1179680 | tf_op jit(solution)/shard_map/ppermute | solution.py:386
  125.4 5.7 all-to-all-start.2
  131.0 2.4 bitcast_dynamic-update-slice_fusion.6
  133.4 2.4 bitcast_dynamic-update-slice_fusion.5
  137.7 13.4 %shift_fwd.1.k_ref = bf16[2048,192]{1,0:T(8,128)(2,1)} custom-call(s32[2176]{0:T(1024)} %copy-done.43, bf16[2048,192]{1,0:T(8,128)(2,1)} %bitcast.352, bf16[64,192]{1,0:T(8,128)(2,1)} %broadcast_in_dim.252.halo_ref, f32[2,64,128]{2,1,0:T(8,128)} %bitcast_bitcast_fusion.taps_ref, s32[2112,1]{1,0:T(8,128)} %broadcast_in_dim.297.segcol_ref), custom_call_target="tpu_custom_call" | custom-call | tf_op jit(solution)/shard_map/shift_fwd/pallas_call | solution.py:90
  154.6 24.8 %mix_fwd.1 = bf16[2048,192]{1,0:T(8,128)(2,1)} custom-call(s32[36,2]{1,0:T(8,128)} %constant.245.clone.tab, bf16[2048,192]{1,0:T(8,128)(2,1)} %bitcast.348, bf16[2048,192]{1,0:T(8,128)(2,1)} %shift_fwd.1.k_ref, bf16[2048,192]{1,0:T(8,128)(2,1)} %bitcast.350, f32[3,1,2560]{2,1,0:T(1,128)} %get-tuple-element.142.row_ref, s32[2048,1]{1,0:T(8,128)} %copy.145.segq_ref.segk_ref, ...), custom_call_target="tpu_custom_call" | custom-call | tf_op jit(solution)/shard_map/mix_fwd/pallas_call | solution.py:263
  181.7 6.2 all-to-all-start.3
  187.9 2.4 bitcast_dynamic-update-slice_fusion.2
  190.3 2.4 bitcast_dynamic-update-slice_fusion.1
  195.1 2.4 bitcast_dynamic-update-slice_fusion.4
  197.5 10.9 %all-to-all-done.3 = bf16[8,256,192]{1,2,0:T(8,128)(2,1)S(1)} async-done(((bf16[8,256,192]{1,2,0:T(8,128)(2,1)}), bf16[8,256,192]{1,2,0:T(8,128)(2,1)S(1)}, u32[]{:S(2)}, u32[]{:S(2)}) %all-to-all-start.3) | async-done | bytes 786464 | tf_op jit(solution)/shard_map/all_to_all | solution.py:457
  212.5 5.6 fusion.14
  218.1 6.1 fusion.6
  224.2 3.5 multiply_reduce_fusion
  232.1 3.0 convolution_convert_fusion
  237.4 3.3 reshape.701
  242.8 4.2 all-to-all-start.4
  251.7 8.4 %collective-permute-done.28 = bf16[192,768]{1,0:T(8,128)(2,1)} collective-permute-done((bf16[192,768]{1,0:T(8,128)(2,1)}, bf16[192,768]{1,0:T(8,128)(2,1)}, u32[]{:S(2)}, u32[]{:S(2)}) %collective-permute-start.28) | collective-permute-done | bytes 294944 | tf_op jit(solution)/shard_map/ppermute | solution.py:386
  262.0 6.1 all-to-all-done.4
  268.1 4.1 all-to-all-start.14
  274.4 46.5 %mix_bwd.1 = (bf16[2048,192]{1,0:T(8,128)(2,1)}, f32[2048,192]{1,0:T(8,128)}, bf16[2048,192]{1,0:T(8,128)(2,1)}, f32[3,1,2560]{2,1,0:T(1,128)}) custom-call(s32[36,2]{1,0:T(8,128)} %constant.245.clone.tab, bf16[2048,192]{1,0:T(8,128)(2,1)} %bitcast.349, bf16[2048,192]{1,0:T(8,128)(2,1)} %shift_fwd.1.k_ref, bf16[2048,192]{1,0:T(8,128)(2,1)} %bitcast.351, ...), custom_call_target="tpu_custom_call" | custom-call | tf_op jit(solution)/shard_map/mix_bwd/pallas_call | solution.py:356
  323.1 5.9 all-to-all-start.5
  331.0 24.8 %shift_bwd.1 = (bf16[2048,192]{1,0:T(8,128)(2,1)}, f32[64,192]{1,0:T(8,128)}) custom-call(s32[2176]{0:T(1024)} %copy-done.43, bf16[2048,192]{1,0:T(8,128)(2,1)} %bitcast.353, bf16[64,192]{1,0:T(8,128)(2,1)} %broadcast_in_dim.252.halo_ref, f32[2048,192]{1,0:T(8,128)} %get-tuple-element.24.g_ref, f32[64,192]{1,0:T(8,128)} %broadcast_in_dim.279.ghalo_ref, ...), custom_call_target="tpu_custom_call" | custom-call | tf_op jit(solution)/shard_map/shift_bwd/pallas_call | solution.py:171
  358.1 6.0 all-to-all-start.6
  366.9 17.1 %all-to-all-done.6 = bf16[8,256,192]{1,2,0:T(8,128)(2,1)} async-done(((bf16[8,256,192]{1,2,0:T(8,128)(2,1)}), bf16[8,256,192]{1,2,0:T(8,128)(2,1)}, u32[]{:S(2)}, u32[]{:S(2)}) %all-to-all-start.6) | async-done | bytes 786464 | tf_op jit(solution)/shard_map/all_to_all | solution.py:457
  384.0 4.4 all-to-all-start.7
  388.4 5.2 fusion.115
  393.7 3.7 copy-done.9
  399.1 4.6 copy.175
  415.5 6.2 all-to-all-start.15
  439.3 5.9 collective-permute-done.22
  446.0 5.8 all-to-all-start.8
  456.7 4.1 all-to-all-done.8
  460.8 3.6 all-to-all-start.10
  464.4 4.5 fusion.124
  468.9 3.6 copy-done.10
  474.9 6.0 all-to-all-start.12
  480.9 3.7 bitcast_add_fusion.1
  487.9 3.3 all-to-all-done.12
  492.0 3.6 all-to-all-start.9
  496.6 8.8 %all-to-all-done.9 = bf16[8,24,768]{2,1,0:T(8,128)(2,1)S(1)} async-done(((bf16[8,24,768]{2,1,0:T(8,128)(2,1)}), bf16[8,24,768]{2,1,0:T(8,128)(2,1)S(1)}, u32[]{:S(2)}, u32[]{:S(2)}) %all-to-all-start.9) | async-done | bytes 294944 | tf_op jit(solution)/shard_map/all_to_all | solution.py:416
  506.1 3.6 all-to-all-start.11
  510.8 8.2 %all-to-all-done.11 = bf16[8,24,768]{2,1,0:T(8,128)(2,1)S(1)} async-done(((bf16[8,24,768]{2,1,0:T(8,128)(2,1)}), bf16[8,24,768]{2,1,0:T(8,128)(2,1)S(1)}, u32[]{:S(2)}, u32[]{:S(2)}) %all-to-all-start.11) | async-done | bytes 294944 | tf_op jit(solution)/shard_map/all_to_all | solution.py:416
  519.7 3.9 all-to-all-start.13
  523.6 3.0 fusion.22
  526.6 6.1 all-to-all-done.13
  532.7 3.6 all-to-all-start.16
  536.4 3.5 bitcast_add_fusion
  540.9 26.2 %collective-permute-done.32 = bf16[768,768]{1,0:T(8,128)(2,1)S(1)} collective-permute-done((bf16[768,768]{1,0:T(8,128)(2,1)S(1)}, bf16[768,768]{1,0:T(8,128)(2,1)S(1)}, u32[]{:S(2)}, u32[]{:S(2)}) %collective-permute-start.32) | collective-permute-done | bytes 1179680 | tf_op jit(solution)/shard_map/ppermute | solution.py:386
  568.4 5.7 all-to-all-start.18
  574.3 26.7 %all-to-all-done.18 = bf16[8,96,768]{2,1,0:T(8,128)(2,1)S(1)} async-done(((bf16[8,96,768]{2,1,0:T(8,128)(2,1)}), bf16[8,96,768]{2,1,0:T(8,128)(2,1)S(1)}, u32[]{:S(2)}, u32[]{:S(2)}) %all-to-all-start.18) | async-done | bytes 1179680 | tf_op jit(solution)/shard_map/all_to_all | solution.py:414
  602.4 3.6 all-to-all-start.17
  607.9 8.8 %add_convert_fusion.1 = bf16[512,768]{1,0:T(8,128)(2,1)} fusion(f32[512,768]{1,0:T(8,128)S(1)} %copy-done.8, bf16[3072,768]{1,0:T(8,128)(2,1)} %bitcast.358, f32[512,3072]{1,0:T(8,128)} %copy-done.89), kind=kOutput, calls=%fused_computation.63 | convolution fusion | flops 2430861312 | bytes 13369344 | tf_op jit(solution)/shard_map/dot_general | solution.py:34
  617.0 5.0 fusion.56
  622.6 12.0 %all-to-all-done.17 = bf16[8,24,3072]{2,1,0:T(8,128)(2,1)S(1)} async-done(((bf16[8,24,3072]{2,1,0:T(8,128)(2,1)}), bf16[8,24,3072]{2,1,0:T(8,128)(2,1)S(1)}, u32[]{:S(2)}, u32[]{:S(2)}) %all-to-all-start.17) | async-done | bytes 1179680 | tf_op jit(solution)/shard_map/all_to_all | solution.py:416
  635.7 3.8 all-to-all-start.19
  642.5 133.9 %all-reduce.6.cloned.1.call-done = f32[4,13443]{1,0:T(4,128)} async-done(((f32[4,13443]{1,0:T(4,128)}), f32[4,13443]{1,0:T(4,128)}) %all-reduce.6.cloned.1.call-update) | async-done | bytes 215104 | tf_op jit(solution)/shard_map/psum | solution.py:597
  (443 shorter events, 184.4 us)
Async XLA Ops:
  7.2 17.5 %copy-start = (s32[2,2048]{1,0:T(2,128)S(1)}, s32[2,2048]{1,0:T(2,128)}, u32[]{:S(2)}) copy-start(s32[2,2048]{1,0:T(2,128)} %param.21) | copy-start | bytes 49156
  14.5 22.4 %collective-permute-start = (bf16[112,128]{1,0:T(8,128)(2,1)}, bf16[112,128]{1,0:T(8,128)(2,1)}, u32[]{:S(2)}, u32[]{:S(2)}) collective-permute-start(bf16[112,128]{1,0:T(8,128)(2,1)} %pad_bitcast_fusion), channel_id=1, source_target_pairs={{0,8},{8,0},{16,24},{24,16},{1,9},{9,1},{17,25},{25,17},{2,10},{10... | collective-permute-start | bytes 86024 | tf_op jit(solution)/shard_map/ppermute | solution.py:386
  15.0 23.7 %collective-permute-start.1 = (bf16[112,128]{1,0:T(8,128)(2,1)}, bf16[112,128]{1,0:T(8,128)(2,1)}, u32[]{:S(2)}, u32[]{:S(2)}) collective-permute-start(bf16[112,128]{1,0:T(8,128)(2,1)} %pad_bitcast_fusion), channel_id=1, source_target_pairs={{0,16},{8,24},{16,0},{24,8},{1,17},{9,25},{17,1},{25,9},{2,18},{10... | collective-permute-start | bytes 86024 | tf_op jit(solution)/shard_map/ppermute | solution.py:386
  17.5 34.0 %collective-permute-start.3 = (bf16[192,768]{1,0:T(8,128)(2,1)}, bf16[192,768]{1,0:T(8,128)(2,1)}, u32[]{:S(2)}, u32[]{:S(2)}) collective-permute-start(bf16[192,768]{1,0:T(8,128)(2,1)} %param.24), channel_id=1, source_target_pairs={{0,8},{8,0},{16,24},{24,16},{1,9},{9,1},{17,25},{25,17},{2,10},{10... | collective-permute-start | bytes 884744 | tf_op jit(solution)/shard_map/ppermute | solution.py:386
  17.7 34.2 %collective-permute-start.4 = (bf16[192,768]{1,0:T(8,128)(2,1)}, bf16[192,768]{1,0:T(8,128)(2,1)}, u32[]{:S(2)}, u32[]{:S(2)}) collective-permute-start(bf16[192,768]{1,0:T(8,128)(2,1)} %param.24), channel_id=1, source_target_pairs={{0,16},{8,24},{16,0},{24,8},{1,17},{9,25},{17,1},{25,9},{2,18},{10... | collective-permute-start | bytes 884744 | tf_op jit(solution)/shard_map/ppermute | solution.py:386
  18.0 47.8 %collective-permute-start.12 = (bf16[192,768]{1,0:T(8,128)(2,1)}, bf16[192,768]{1,0:T(8,128)(2,1)}, u32[]{:S(2)}, u32[]{:S(2)}) collective-permute-start(bf16[192,768]{1,0:T(8,128)(2,1)} %param.32), channel_id=1, source_target_pairs={{0,8},{8,0},{16,24},{24,16},{1,9},{9,1},{17,25},{25,17},{2,10},{10... | collective-permute-start | bytes 884744 | tf_op jit(solution)/shard_map/ppermute | solution.py:386
  34.1 16.3 %copy-start.43 = (s32[2176]{0:T(1024)}, s32[2176]{0:T(1024)S(1)}, u32[]{:S(2)}) copy-start(s32[2176]{0:T(1024)S(1)} %fusion.87.seg_s) | copy-start | bytes 26116
  36.9 32.1 %collective-permute-start.13 = (bf16[192,768]{1,0:T(8,128)(2,1)}, bf16[192,768]{1,0:T(8,128)(2,1)}, u32[]{:S(2)}, u32[]{:S(2)}) collective-permute-start(bf16[192,768]{1,0:T(8,128)(2,1)} %param.32), channel_id=1, source_target_pairs={{0,16},{8,24},{16,0},{24,8},{1,17},{9,25},{17,1},{25,9},{2,18},{10... | collective-permute-start | bytes 884744 | tf_op jit(solution)/shard_map/ppermute | solution.py:386
  38.7 1.7 collective-permute-start.2
  40.4 30.8 %collective-permute-start.6 = (bf16[192,768]{1,0:T(8,128)(2,1)}, bf16[192,768]{1,0:T(8,128)(2,1)}, u32[]{:S(2)}, u32[]{:S(2)}) collective-permute-start(bf16[192,768]{1,0:T(8,128)(2,1)} %param.25), channel_id=1, source_target_pairs={{0,8},{8,0},{16,24},{24,16},{1,9},{9,1},{17,25},{25,17},{2,10},{10... | collective-permute-start | bytes 884744 | tf_op jit(solution)/shard_map/ppermute | solution.py:386
  51.5 19.8 %collective-permute-start.7 = (bf16[192,768]{1,0:T(8,128)(2,1)}, bf16[192,768]{1,0:T(8,128)(2,1)}, u32[]{:S(2)}, u32[]{:S(2)}) collective-permute-start(bf16[192,768]{1,0:T(8,128)(2,1)} %param.25), channel_id=1, source_target_pairs={{0,16},{8,24},{16,0},{24,8},{1,17},{9,25},{17,1},{25,9},{2,18},{10... | collective-permute-start | bytes 884744 | tf_op jit(solution)/shard_map/ppermute | solution.py:386
  51.9 2.0 collective-permute-start.5
  53.9 45.8 %collective-permute-start.9 = (bf16[192,768]{1,0:T(8,128)(2,1)}, bf16[192,768]{1,0:T(8,128)(2,1)}, u32[]{:S(2)}, u32[]{:S(2)}) collective-permute-start(bf16[192,768]{1,0:T(8,128)(2,1)} %param.26), channel_id=1, source_target_pairs={{0,8},{8,0},{16,24},{24,16},{1,9},{9,1},{17,25},{25,17},{2,10},{10... | collective-permute-start | bytes 884744 | tf_op jit(solution)/shard_map/ppermute | solution.py:386
  59.7 26.4 %all-to-all-start = ((bf16[8,256,192]{1,2,0:T(8,128)(2,1)}), bf16[8,256,192]{1,2,0:T(8,128)(2,1)S(1)}, u32[]{:S(2)}, u32[]{:S(2)}) async-start(bf16[8,256,192]{1,2,0:T(8,128)(2,1)} %bitcast.13), calls=%async_computation | async-start | bytes 1572864 | tf_op jit(solution)/shard_map/all_to_all | solution.py:457
  65.8 33.9 %collective-permute-start.10 = (bf16[192,768]{1,0:T(8,128)(2,1)}, bf16[192,768]{1,0:T(8,128)(2,1)}, u32[]{:S(2)}, u32[]{:S(2)}) collective-permute-start(bf16[192,768]{1,0:T(8,128)(2,1)} %param.26), channel_id=1, source_target_pairs={{0,16},{8,24},{16,0},{24,8},{1,17},{9,25},{17,1},{25,9},{2,18},{10... | collective-permute-start | bytes 884744 | tf_op jit(solution)/shard_map/ppermute | solution.py:386
  69.1 42.7 %collective-permute-start.19 = (bf16[768,768]{1,0:T(8,128)(2,1)}, bf16[768,768]{1,0:T(8,128)(2,1)}, u32[]{:S(2)}, u32[]{:S(2)}) collective-permute-start(bf16[768,768]{1,0:T(8,128)(2,1)} %param.36), channel_id=1, source_target_pairs={{0,16},{8,24},{16,0},{24,8},{1,17},{9,25},{17,1},{25,9},{2,18},{10... | collective-permute-start | bytes 3538952 | tf_op jit(solution)/shard_map/ppermute | solution.py:386
  71.3 3.9 collective-permute-start.14
  71.3 4.0 collective-permute-start.8
  75.2 55.9 %collective-permute-start.15 = (bf16[192,3072]{1,0:T(8,128)(2,1)}, bf16[192,3072]{1,0:T(8,128)(2,1)}, u32[]{:S(2)}, u32[]{:S(2)}) collective-permute-start(bf16[192,3072]{1,0:T(8,128)(2,1)} %param.35), channel_id=1, source_target_pairs={{0,8},{8,0},{16,24},{24,16},{1,9},{9,1},{17,25},{25,17},{2,10},{10... | collective-permute-start | bytes 3538952 | tf_op jit(solution)/shard_map/ppermute | solution.py:386
  75.3 50.1 %collective-permute-start.16 = (bf16[192,3072]{1,0:T(8,128)(2,1)}, bf16[192,3072]{1,0:T(8,128)(2,1)}, u32[]{:S(2)}, u32[]{:S(2)}) collective-permute-start(bf16[192,3072]{1,0:T(8,128)(2,1)} %param.35), channel_id=1, source_target_pairs={{0,16},{8,24},{16,0},{24,8},{1,17},{9,25},{17,1},{25,9},{2,18},{10... | collective-permute-start | bytes 3538952 | tf_op jit(solution)/shard_map/ppermute | solution.py:386
  86.2 39.2 %all-to-all-start.1 = ((bf16[8,256,192]{1,2,0:T(8,128)(2,1)}), bf16[8,256,192]{1,2,0:T(8,128)(2,1)S(1)}, u32[]{:S(2)}, u32[]{:S(2)}) async-start(bf16[8,256,192]{1,2,0:T(8,128)(2,1)} %bitcast.369), calls=%async_computation.1 | async-start | bytes 1572864 | tf_op jit(solution)/shard_map/all_to_all | solution.py:457
  98.2 129.6 %copy-start.66 = (f32[768]{0:T(1024)}, f32[768]{0:T(1024)S(1)}, u32[]{:S(2)}) copy-start(f32[768]{0:T(1024)S(1)} %reshape.736) | copy-start | bytes 9220
  99.7 88.3 %collective-permute-start.18 = (bf16[768,768]{1,0:T(8,128)(2,1)}, bf16[768,768]{1,0:T(8,128)(2,1)}, u32[]{:S(2)}, u32[]{:S(2)}) collective-permute-start(bf16[768,768]{1,0:T(8,128)(2,1)} %param.36), channel_id=1, source_target_pairs={{0,8},{8,0},{16,24},{24,16},{1,9},{9,1},{17,25},{25,17},{2,10},{10... | collective-permute-start | bytes 3538952 | tf_op jit(solution)/shard_map/ppermute | solution.py:386
  99.7 3.1 collective-permute-start.11
  111.8 80.9 %collective-permute-start.20 = (bf16[768,768]{1,0:T(8,128)(2,1)}, bf16[768,768]{1,0:T(8,128)(2,1)}, u32[]{:S(2)}, u32[]{:S(2)}) collective-permute-start(bf16[768,768]{1,0:T(8,128)(2,1)} %collective-permute-done.19), channel_id=1, source_target_pairs={{0,8},{8,0},{16,24},{24,16},{1,9},{9,1},{17,25},{25,17},{2,10},{10... | collective-permute-start | bytes 3538952 | tf_op jit(solution)/shard_map/ppermute | solution.py:386
  125.4 69.7 %collective-permute-start.17 = (bf16[192,3072]{1,0:T(8,128)(2,1)}, bf16[192,3072]{1,0:T(8,128)(2,1)}, u32[]{:S(2)}, u32[]{:S(2)}) collective-permute-start(bf16[192,3072]{1,0:T(8,128)(2,1)} %collective-permute-done.16), channel_id=1, source_target_pairs={{0,8},{8,0},{16,24},{24,16},{1,9},{9,1},{17,25},{25,17},{2,10},{10... | collective-permute-start | bytes 3538952 | tf_op jit(solution)/shard_map/ppermute | solution.py:386
  125.4 27.0 %all-to-all-start.2 = ((bf16[8,256,192]{1,2,0:T(8,128)(2,1)}), bf16[8,256,192]{1,2,0:T(8,128)(2,1)}, u32[]{:S(2)}, u32[]{:S(2)}) async-start(bf16[8,256,192]{1,2,0:T(8,128)(2,1)} %bitcast.371), calls=%async_computation.2 | async-start | bytes 1572864 | tf_op jit(solution)/shard_map/all_to_all | solution.py:457
  181.7 26.7 %all-to-all-start.3 = ((bf16[8,256,192]{1,2,0:T(8,128)(2,1)}), bf16[8,256,192]{1,2,0:T(8,128)(2,1)S(1)}, u32[]{:S(2)}, u32[]{:S(2)}) async-start(bf16[8,256,192]{1,2,0:T(8,128)(2,1)} %copy.146), calls=%async_computation.3 | async-start | bytes 1572864 | tf_op jit(solution)/shard_map/all_to_all | solution.py:457
  232.1 14.9 %collective-permute-start.27 = (bf16[2,192,768]{2,1,0:T(8,128)(2,1)}, bf16[2,192,768]{2,1,0:T(8,128)(2,1)}, u32[]{:S(2)}, u32[]{:S(2)}) collective-permute-start(bf16[2,192,768]{2,1,0:T(8,128)(2,1)} %fusion.77), channel_id=1, source_target_pairs={{0,8},{8,0},{16,24},{24,16},{1,9},{9,1},{17,25},{25,17},{2,10},{10... | collective-permute-start | bytes 1769480 | tf_op jit(solution)/shard_map/ppermute | solution.py:386
  242.8 25.3 %all-to-all-start.4 = ((bf16[8,256,192]{1,2,0:T(8,128)(2,1)}), bf16[8,256,192]{1,2,0:T(8,128)(2,1)}, u32[]{:S(2)}, u32[]{:S(2)}) async-start(bf16[8,256,192]{1,2,0:T(8,128)(2,1)} %bitcast.370), calls=%async_computation.4 | async-start | bytes 1572864 | tf_op jit(solution)/shard_map/all_to_all | solution.py:457
  250.4 9.7 %collective-permute-start.28 = (bf16[192,768]{1,0:T(8,128)(2,1)}, bf16[192,768]{1,0:T(8,128)(2,1)}, u32[]{:S(2)}, u32[]{:S(2)}) collective-permute-start(bf16[192,768]{1,0:T(8,128)(2,1)} %fusion.85), channel_id=1, source_target_pairs={{0,16},{8,24},{16,0},{24,8},{1,17},{9,25},{17,1},{25,9},{2,18},{10... | collective-permute-start | bytes 884744 | tf_op jit(solution)/shard_map/ppermute | solution.py:386
  268.1 55.0 %all-to-all-start.14 = ((bf16[8,24,768]{2,1,0:T(8,128)(2,1)}), bf16[8,24,768]{2,1,0:T(8,128)(2,1)}, u32[]{:S(2)}, u32[]{:S(2)}) async-start(bf16[8,24,768]{2,1,0:T(8,128)(2,1)} %bitcast.394), calls=%async_computation.14 | async-start | bytes 589824 | tf_op jit(solution)/shard_map/all_to_all | solution.py:414
  323.1 35.0 %all-to-all-start.5 = ((bf16[8,256,192]{1,2,0:T(8,128)(2,1)}), bf16[8,256,192]{1,2,0:T(8,128)(2,1)}, u32[]{:S(2)}, u32[]{:S(2)}) async-start(bf16[8,256,192]{1,2,0:T(8,128)(2,1)} %copy.153), calls=%async_computation.5 | async-start | bytes 1572864 | tf_op jit(solution)/shard_map/all_to_all | solution.py:457
  358.1 25.9 %all-to-all-start.6 = ((bf16[8,256,192]{1,2,0:T(8,128)(2,1)}), bf16[8,256,192]{1,2,0:T(8,128)(2,1)}, u32[]{:S(2)}, u32[]{:S(2)}) async-start(bf16[8,256,192]{1,2,0:T(8,128)(2,1)} %copy.156), calls=%async_computation.6 | async-start | bytes 1572864 | tf_op jit(solution)/shard_map/all_to_all | solution.py:457
  364.7 23.7 %copy-start.59 = (f32[512]{0:T(512)S(1)}, f32[512]{0:T(512)}, u32[]{:S(2)}) copy-start(f32[512]{0:T(512)} %copy-done.58) | copy-start | bytes 6148
  364.7 23.7 %copy-start.67 = (f32[768]{0:T(1024)S(1)}, f32[768]{0:T(1024)}, u32[]{:S(2)}) copy-start(f32[768]{0:T(1024)} %copy-done.66) | copy-start | bytes 9220
  384.0 30.0 %all-to-all-start.7 = ((bf16[8,256,192]{1,2,0:T(8,128)(2,1)}), bf16[8,256,192]{1,2,0:T(8,128)(2,1)}, u32[]{:S(2)}, u32[]{:S(2)}) async-start(bf16[8,256,192]{1,2,0:T(8,128)(2,1)} %copy.158), calls=%async_computation.7 | async-start | bytes 1572864 | tf_op jit(solution)/shard_map/all_to_all | solution.py:457
  399.1 81.8 %collective-permute-start.29 = (bf16[2,192,3072]{2,1,0:T(8,128)(2,1)}, bf16[2,192,3072]{2,1,0:T(8,128)(2,1)}, u32[]{:S(2)}, u32[]{:S(2)}) collective-permute-start(bf16[2,192,3072]{2,1,0:T(8,128)(2,1)} %fusion.19), channel_id=1, source_target_pairs={{0,8},{8,0},{16,24},{24,16},{1,9},{9,1},{17,25},{25,17},{2,10},{10... | collective-permute-start | bytes 7077896 | tf_op jit(solution)/shard_map/ppermute | solution.py:386
  415.5 30.5 %all-to-all-start.15 = ((bf16[8,24,768]{2,1,0:T(8,128)(2,1)}), bf16[8,24,768]{2,1,0:T(8,128)(2,1)}, u32[]{:S(2)}, u32[]{:S(2)}) async-start(bf16[8,24,768]{2,1,0:T(8,128)(2,1)} %broadcast_in_dim.294), calls=%async_computation.15 | async-start | bytes 589824 | tf_op jit(solution)/shard_map/all_to_all | solution.py:416
  431.0 4.2 collective-permute-start.21
  432.9 3.3 collective-permute-start.23
  434.9 16.9 %collective-permute-start.25 = (bf16[2,192,768]{2,1,0:T(8,128)(2,1)S(1)}, bf16[2,192,768]{2,1,0:T(8,128)(2,1)}, u32[]{:S(2)}, u32[]{:S(2)}) collective-permute-start(bf16[2,192,768]{2,1,0:T(8,128)(2,1)S(1)} %fusion.76), channel_id=1, source_target_pairs={{0,8},{8,0},{16,24},{24,16},{1,9},{9,1},{17,25},{25,17},{2,10},{10... | collective-permute-start | bytes 1769480 | tf_op jit(solution)/shard_map/ppermute | solution.py:386
  435.3 9.9 %collective-permute-start.22 = (bf16[192,768]{1,0:T(8,128)(2,1)S(1)}, bf16[192,768]{1,0:T(8,128)(2,1)S(1)}, u32[]{:S(2)}, u32[]{:S(2)}) collective-permute-start(bf16[192,768]{1,0:T(8,128)(2,1)S(1)} %fusion.82), channel_id=1, source_target_pairs={{0,16},{8,24},{16,0},{24,8},{1,17},{9,25},{17,1},{25,9},{2,18},{10... | collective-permute-start | bytes 884744 | tf_op jit(solution)/shard_map/ppermute | solution.py:386
  438.1 16.9 %collective-permute-start.24 = (bf16[192,768]{1,0:T(8,128)(2,1)}, bf16[192,768]{1,0:T(8,128)(2,1)}, u32[]{:S(2)}, u32[]{:S(2)}) collective-permute-start(bf16[192,768]{1,0:T(8,128)(2,1)} %fusion.83), channel_id=1, source_target_pairs={{0,16},{8,24},{16,0},{24,8},{1,17},{9,25},{17,1},{25,9},{2,18},{10... | collective-permute-start | bytes 884744 | tf_op jit(solution)/shard_map/ppermute | solution.py:386
  446.0 14.8 %all-to-all-start.8 = ((bf16[8,24,768]{2,1,0:T(8,128)(2,1)}), bf16[8,24,768]{2,1,0:T(8,128)(2,1)S(1)}, u32[]{:S(2)}, u32[]{:S(2)}) async-start(bf16[8,24,768]{2,1,0:T(8,128)(2,1)} %bitcast.81), calls=%async_computation.8 | async-start | bytes 589824 | tf_op jit(solution)/shard_map/all_to_all | solution.py:414
  454.1 20.1 %collective-permute-start.26 = (bf16[192,768]{1,0:T(8,128)(2,1)S(1)}, bf16[192,768]{1,0:T(8,128)(2,1)S(1)}, u32[]{:S(2)}, u32[]{:S(2)}) collective-permute-start(bf16[192,768]{1,0:T(8,128)(2,1)S(1)} %fusion.84), channel_id=1, source_target_pairs={{0,16},{8,24},{16,0},{24,8},{1,17},{9,25},{17,1},{25,9},{2,18},{10... | collective-permute-start | bytes 884744 | tf_op jit(solution)/shard_map/ppermute | solution.py:386
  460.8 14.2 %all-to-all-start.10 = ((bf16[8,24,768]{2,1,0:T(8,128)(2,1)}), bf16[8,24,768]{2,1,0:T(8,128)(2,1)S(1)}, u32[]{:S(2)}, u32[]{:S(2)}) async-start(bf16[8,24,768]{2,1,0:T(8,128)(2,1)} %bitcast.88), calls=%async_computation.10 | async-start | bytes 589824 | tf_op jit(solution)/shard_map/all_to_all | solution.py:414
  474.2 62.2 %collective-permute-start.31 = (bf16[2,768,768]{2,1,0:T(8,128)(2,1)}, bf16[2,768,768]{2,1,0:T(8,128)(2,1)}, u32[]{:S(2)}, u32[]{:S(2)}) collective-permute-start(bf16[2,768,768]{2,1,0:T(8,128)(2,1)} %fusion.20), channel_id=1, source_target_pairs={{0,8},{8,0},{16,24},{24,16},{1,9},{9,1},{17,25},{25,17},{2,10},{10... | collective-permute-start | bytes 7077896 | tf_op jit(solution)/shard_map/ppermute | solution.py:386
  474.9 16.2 %all-to-all-start.12 = ((bf16[8,24,768]{2,1,0:T(8,128)(2,1)}), bf16[8,24,768]{2,1,0:T(8,128)(2,1)S(1)}, u32[]{:S(2)}, u32[]{:S(2)}) async-start(bf16[8,24,768]{2,1,0:T(8,128)(2,1)} %bitcast.95), calls=%async_computation.12 | async-start | bytes 589824 | tf_op jit(solution)/shard_map/all_to_all | solution.py:414
  487.0 36.6 %collective-permute-start.30 = (bf16[192,3072]{1,0:T(8,128)(2,1)S(1)}, bf16[192,3072]{1,0:T(8,128)(2,1)S(1)}, u32[]{:S(2)}, u32[]{:S(2)}) collective-permute-start(bf16[192,3072]{1,0:T(8,128)(2,1)S(1)} %fusion.44), channel_id=1, source_target_pairs={{0,16},{8,24},{16,0},{24,8},{1,17},{9,25},{17,1},{25,9},{2,18},{10... | collective-permute-start | bytes 3538952 | tf_op jit(solution)/shard_map/ppermute | solution.py:386
  492.0 13.4 %all-to-all-start.9 = ((bf16[8,24,768]{2,1,0:T(8,128)(2,1)}), bf16[8,24,768]{2,1,0:T(8,128)(2,1)S(1)}, u32[]{:S(2)}, u32[]{:S(2)}) async-start(bf16[8,24,768]{2,1,0:T(8,128)(2,1)} %broadcast_in_dim.291), calls=%async_computation.9 | async-start | bytes 589824 | tf_op jit(solution)/shard_map/all_to_all | solution.py:416
  506.1 12.8 %all-to-all-start.11 = ((bf16[8,24,768]{2,1,0:T(8,128)(2,1)}), bf16[8,24,768]{2,1,0:T(8,128)(2,1)S(1)}, u32[]{:S(2)}, u32[]{:S(2)}) async-start(bf16[8,24,768]{2,1,0:T(8,128)(2,1)} %broadcast_in_dim.292), calls=%async_computation.11 | async-start | bytes 589824 | tf_op jit(solution)/shard_map/all_to_all | solution.py:416
  519.7 13.0 %all-to-all-start.13 = ((bf16[8,24,768]{2,1,0:T(8,128)(2,1)}), bf16[8,24,768]{2,1,0:T(8,128)(2,1)S(1)}, u32[]{:S(2)}, u32[]{:S(2)}) async-start(bf16[8,24,768]{2,1,0:T(8,128)(2,1)} %broadcast_in_dim.293), calls=%async_computation.13 | async-start | bytes 589824 | tf_op jit(solution)/shard_map/all_to_all | solution.py:416
  532.7 35.7 %all-to-all-start.16 = ((bf16[8,24,3072]{2,1,0:T(8,128)(2,1)}), bf16[8,24,3072]{2,1,0:T(8,128)(2,1)S(1)}, u32[]{:S(2)}, u32[]{:S(2)}) async-start(bf16[8,24,3072]{2,1,0:T(8,128)(2,1)} %bitcast.115), calls=%async_computation.16 | async-start | bytes 2359296 | tf_op jit(solution)/shard_map/all_to_all | solution.py:414
  540.1 27.1 %collective-permute-start.32 = (bf16[768,768]{1,0:T(8,128)(2,1)S(1)}, bf16[768,768]{1,0:T(8,128)(2,1)S(1)}, u32[]{:S(2)}, u32[]{:S(2)}) collective-permute-start(bf16[768,768]{1,0:T(8,128)(2,1)S(1)} %fusion.45), channel_id=1, source_target_pairs={{0,16},{8,24},{16,0},{24,8},{1,17},{9,25},{17,1},{25,9},{2,18},{10... | collective-permute-start | bytes 3538952 | tf_op jit(solution)/shard_map/ppermute | solution.py:386
  568.4 32.6 %all-to-all-start.18 = ((bf16[8,96,768]{2,1,0:T(8,128)(2,1)}), bf16[8,96,768]{2,1,0:T(8,128)(2,1)S(1)}, u32[]{:S(2)}, u32[]{:S(2)}) async-start(bf16[8,96,768]{2,1,0:T(8,128)(2,1)} %bitcast.125), calls=%async_computation.18 | async-start | bytes 2359296 | tf_op jit(solution)/shard_map/all_to_all | solution.py:414
  574.3 32.2 %copy-start.77 = (f32[768]{0:T(1024)S(1)}, f32[768]{0:T(1024)}, u32[]{:S(2)}) copy-start(f32[768]{0:T(1024)} %get-tuple-element.97) | copy-start | bytes 9220
  574.3 32.9 %copy-start.76 = (f32[768]{0:T(1024)S(1)}, f32[768]{0:T(1024)}, u32[]{:S(2)}) copy-start(f32[768]{0:T(1024)} %get-tuple-element.101) | copy-start | bytes 9220
  574.3 33.5 %copy-start.8 = (f32[512,768]{1,0:T(8,128)S(1)}, f32[512,768]{1,0:T(8,128)}, u32[]{:S(2)}) copy-start(f32[512,768]{1,0:T(8,128)} %copy-done.7) | copy-start | bytes 4718596
  602.4 32.2 %all-to-all-start.17 = ((bf16[8,24,3072]{2,1,0:T(8,128)(2,1)}), bf16[8,24,3072]{2,1,0:T(8,128)(2,1)S(1)}, u32[]{:S(2)}, u32[]{:S(2)}) async-start(bf16[8,24,3072]{2,1,0:T(8,128)(2,1)} %broadcast_in_dim.295), calls=%async_computation.17 | async-start | bytes 2359296 | tf_op jit(solution)/shard_map/all_to_all | solution.py:416
  622.6 16.9 %copy-start.87 = (pred[4]{0:T(512)(128)(4,1)S(1)}, pred[4]{0:T(512)(128)(4,1)}, u32[]{:S(2)}) copy-start(pred[4]{0:T(512)(128)(4,1)} %iota_compare_fusion) | copy-start | bytes 16
  635.7 152.4 %all-to-all-start.19 = ((bf16[8,96,768]{2,1,0:T(8,128)(2,1)}), bf16[8,96,768]{2,1,0:T(8,128)(2,1)S(1)}, u32[]{:S(2)}, u32[]{:S(2)}) async-start(bf16[8,96,768]{2,1,0:T(8,128)(2,1)} %broadcast_in_dim.296), calls=%async_computation.19 | async-start | bytes 2359296 | tf_op jit(solution)/shard_map/all_to_all | solution.py:416
  639.5 137.0 %all-reduce.6.cloned.1.call-start = ((), (), s32[]{:S(2)}) async-start(), calls=%async_computation.20 | async-start | bytes 434176 | tf_op jit(solution)/shard_map/psum | solution.py:597
  640.6 144.9 %copy-start.32 = (bf16[8,24,768]{2,1,0:T(8,128)(2,1)S(1)}, bf16[8,24,768]{2,1,0:T(8,128)(2,1)}, u32[]{:S(2)}) copy-start(bf16[8,24,768]{2,1,0:T(8,128)(2,1)} %copy-done.31) | copy-start | bytes 884740
  (82 other events, 438.8 us)
Sparse Core Ops, SparseCore 0:
  646.4 129.9 all-reduce.5
